TPU v7x, 256 devices: a whole 4x4x8 slice. The times are simulated.
256 devices in a mesh: grid: 16 (over z, core), pencil: 16 (over y, x).
Axes of the slice: x: 4, y: 4, z: 8, core: 2. Of those that a mesh axis runs over, the one named last changes fastest.
Arguments:
- field: bfloat16 [16, 512, 256, 128], P('grid', 'pencil'), may hold values from -6 to 6
- levels: int32 [16, 3], P('grid'), may hold values from 7 to 9, as said below
- coefficients: int32 [16], P('grid'), may hold values from -2 to 2
- failed: int32 [16], P('grid'), may hold values 0 or 1
- owner_map: int32 [64], replicated, may hold values from -1 to 47, as said below
- velocity: float32 [3], replicated, may hold values from -1 to 1
- diffusivity: float32 [3], replicated, may hold values from 0.5 to 4
Outputs:
- combined: float32 [48, 2, 128, 4096], P('grid', None, 'pencil')
Inputs may be any that keep to these rules, and one draw needn't show every extreme that they name: `levels`: each row is (9, 8, 7) or (8, 9, 7); each occurs in 8 rows. `owner_map`: blocks held by no grid map to -1; every other block maps to a distinct row, and every row is named once. Owner o holds rows o * 3 to o * 3 + 2: 1 block held by grids of both level vectors and 1 held only by grids of each one, so every grid holds exactly 2 of each owner's blocks.
All inputs are finite; a program needn't handle non-finite values. No bound on the sum of `failed` on one device may be relied on, other than what follows from the above.
Results may differ from a plain program's by a relative error of at most 0.0056.
Values may be sent and summed in bfloat16 or wider, within the bound.
A program may use at most 128 MiB of HBM per device.

v0:
```python
import math

import jax
import jax.numpy as jnp
from jax import lax
from jax.sharding import PartitionSpec as P


def signed_modes(positions, length):
    return jnp.where(positions < length // 2, positions, positions - length).astype(jnp.float32)


def dft_tables(length):
    positions = jnp.arange(length, dtype=jnp.int32)
    product = positions[:, None] * positions[None, :] % length
    angles = product.astype(jnp.float32) * (2.0 * math.pi / length)
    return jnp.stack([jnp.cos(angles), -jnp.sin(angles)]).astype(jnp.bfloat16)


def complex_table(length):
    tables = dft_tables(length)
    return jnp.stack([jnp.stack([tables[0], -tables[1]]), jnp.stack([tables[1], tables[0]])])


def apply_factor(
    spectrum,
    z_modes,
    long_modes,
    mid_modes,
    swapped,
    velocity,
    diffusivity,
    long_len,
    mid_len,
    z_len,
):
    nu_long = jnp.where(swapped, diffusivity[1], diffusivity[0])
    nu_mid = jnp.where(swapped, diffusivity[0], diffusivity[1])
    speed_long = jnp.where(swapped, velocity[1], velocity[0])
    speed_mid = jnp.where(swapped, velocity[0], velocity[1])
    z_grid = z_modes[:, None, None]
    long_grid = long_modes[None, :, None]
    mid_grid = mid_modes[None, None, :]
    exponent = (
        diffusivity[2] * z_grid * z_grid
        + nu_long * long_grid * long_grid
        + nu_mid * mid_grid * mid_grid
    ) * (-4.0 / (long_len * long_len))
    phases = (velocity[2] * z_grid + speed_long * long_grid + speed_mid * mid_grid) * (
        -2.0 * math.pi / mid_len
    )
    magnitude = jnp.exp(exponent) * (1.0 / math.sqrt(long_len * mid_len * z_len))
    factor_re = magnitude * jnp.cos(phases)
    factor_im = magnitude * jnp.sin(phases)
    real_part = spectrum[0] * factor_re - spectrum[1] * factor_im
    imag_part = spectrum[0] * factor_im + spectrum[1] * factor_re
    return jnp.stack([real_part, imag_part])


def block_rows(swapped, owner_map, per_long, per_mid):
    along_long = jnp.arange(per_long, dtype=jnp.int32)[:, None] * jnp.ones((1, per_mid), jnp.int32)
    mid_raw = jnp.arange(per_mid, dtype=jnp.int32)
    mid_global = jnp.where(mid_raw < per_mid // 2, mid_raw, mid_raw + per_long - per_mid)
    along_mid = jnp.ones((per_long, 1), jnp.int32) * mid_global[None, :]
    block_x = jnp.where(swapped, along_mid, along_long)
    block_y = jnp.where(swapped, along_long, along_mid)
    return owner_map[(block_x * per_long + block_y).reshape(-1)]


def turn_inner(grouped):
    return grouped.transpose(0, 1, 2, 3, 5, 4)


def keep_inner(grouped):
    return grouped


def body(field, levels, coefficients, failed, owner_map, velocity, diffusivity):
    samples = field[0]
    local_long, mid_len, z_len = samples.shape
    pencils = lax.axis_size("pencil")
    grid_count = lax.axis_size("grid")
    long_len = local_long * pencils
    z_local = z_len // pencils
    block_len = mid_len // 4
    per_long = long_len // block_len
    per_mid = mid_len // block_len
    swapped = levels[0, 0] < levels[0, 1]
    along_z = jnp.einsum(
        "abc,pck->pabk", samples, dft_tables(z_len), preferred_element_type=jnp.float32
    ).astype(jnp.bfloat16)
    along_mid = jnp.einsum(
        "qabc,pqbd->padc", along_z, complex_table(mid_len), preferred_element_type=jnp.float32
    ).astype(jnp.bfloat16)
    table_long = complex_table(long_len)
    spectrum = jnp.einsum(
        "qabc,pqae->pceb",
        lax.all_to_all(along_mid, "pencil", split_axis=3, concat_axis=1, tiled=True),
        table_long,
        preferred_element_type=jnp.float32,
    )
    z_start = lax.axis_index("pencil") * z_local
    z_modes = signed_modes(z_start + jnp.arange(z_local, dtype=jnp.int32), z_len)
    long_modes = signed_modes(jnp.arange(long_len, dtype=jnp.int32), long_len)
    mid_modes = signed_modes(jnp.arange(mid_len, dtype=jnp.int32), mid_len)
    shifted = apply_factor(
        spectrum,
        z_modes,
        long_modes,
        mid_modes,
        swapped,
        velocity,
        diffusivity,
        long_len,
        mid_len,
        z_len,
    )
    grouped = shifted.reshape(2, z_local, per_long, block_len, per_mid, block_len).transpose(
        2, 4, 0, 1, 3, 5
    )
    turned = lax.cond(swapped, turn_inner, keep_inner, grouped)
    held_count = per_long * per_mid
    blocks = turned.reshape(held_count, 2, z_local, block_len * block_len)
    row_ids = block_rows(swapped, owner_map, per_long, per_mid)
    weight = (coefficients[0] * (1 - failed[0])).astype(jnp.float32)
    weighted = blocks * weight
    slot_count = (2 * held_count - per_mid * per_mid) // grid_count
    capacity = held_count // grid_count
    owners = row_ids // slot_count
    slot_ids = row_ids % slot_count
    positions_all = jnp.arange(held_count, dtype=jnp.int32)
    earlier = (owners[:, None] == owners[None, :]) & (
        positions_all[None, :] < positions_all[:, None]
    )
    rank_in = jnp.sum(earlier.astype(jnp.int32), axis=1)
    target = owners * capacity + rank_in
    outgoing = (
        jnp.zeros_like(weighted)
        .at[target]
        .set(weighted)
        .reshape(grid_count, capacity, 2, z_local, block_len * block_len)
    )
    labels = (
        jnp.zeros((held_count,), jnp.float32)
        .at[target]
        .set(slot_ids.astype(jnp.float32))
        .reshape(grid_count, capacity)
    )
    incoming, got_labels = (
        lax.all_to_all(outgoing, "grid", split_axis=0, concat_axis=0, tiled=True),
        lax.all_to_all(labels, "grid", split_axis=0, concat_axis=0, tiled=True),
    )
    selector = (
        got_labels.reshape(1, -1)
        == jnp.arange(slot_count, dtype=jnp.int32).astype(jnp.float32)[:, None]
    ).astype(jnp.float32)
    combined = jnp.dot(
        selector, incoming.reshape(grid_count * capacity, -1), precision=lax.Precision.HIGHEST
    ).reshape(slot_count, 2, z_local, block_len * block_len)
    return combined


def solution(mesh):
    placed = (P("grid", "pencil", None, None), P("grid", None), P("grid"), P("grid"), P(), P(), P())
    return jax.shard_map(
        body, mesh=mesh, in_specs=placed, out_specs=P("grid", None, "pencil", None), check_vma=False
    )
```

profile of v0, /device:TPU:1, one launch (start us, length us, event | category | flops | bytes accessed | tf_op | source)
XLA Modules:
  0.0 430.6 jit_solution(11301004239120380274)
XLA Ops:
  0.0 0.0 copy-start
  0.0 1.1 negate_convert_fusion.1
  1.1 1.0 fusion.39
  2.1 0.3 negate_convert_fusion.2
  2.4 0.0 copy-done
  2.5 5.0 %fusion.2 = bf16[2,32,256,128]{3,2,1,0:T(8,128)(2,1)} fusion(bf16[1,32,256,128]{3,2,1,0:T(8,128)(2,1)S(1)} %copy-done, bf16[1,2,256,256]{2,3,1,0:T(8,128)(2,1)S(1)} %get-tuple-element.19, bf16[1,2,256,256]{2,3,1,0:T(8,128)(2,1)S(1)} %get-tuple-element.18, bf16[1,128,128]{1,2,0:T(8,128)(2,1)S(1)} %get-tuple-element.31, ...), kind=kOutput, calls=%fused_computation.6 | convolution fusion | flops 2689728512 | bytes 6881280 | tf_op jit(solution)/shard_map/qabc,pqbd->padc/dot_general | solution.py:92
  7.5 7.9 %copy.30 = bf16[2,32,256,128]{2,1,0,3:T(8,128)(2,1)} copy(bf16[2,32,256,128]{3,2,1,0:T(8,128)(2,1)} %fusion.2) | data formatting | bytes 8388608 | tf_op jit(solution)/shard_map/convert_element_type | solution.py:94
  15.4 0.0 copy-start.6
  15.4 0.0 copy-start.4
  15.4 0.0 copy-start.5
  15.4 0.0 copy-start.2
  15.4 7.8 %all-to-all-start.1 = ((bf16[2,32,256,128]{2,1,0,3:T(8,128)(2,1)}), bf16[2,32,256,128]{2,1,0,3:T(8,128)(2,1)}, u32[]{:S(2)}, u32[]{:S(2)}) async-start(bf16[2,32,256,128]{2,1,0,3:T(8,128)(2,1)} %copy.30), calls=%async_computation.1 | async-start | bytes 8388608 | tf_op jit(solution)/shard_map/all_to_all | solution.py:98
  23.2 0.0 copy-done.6
  23.2 0.6 fusion.62
  25.0 0.0 copy-done.4
  25.1 0.6 fusion.61
  28.0 0.0 copy-done.5
  28.1 0.6 fusion.60
  32.5 0.1 add.269
  32.6 0.0 copy-done.2
  32.7 0.7 gather_fusion
  33.4 0.2 convert_reduce_fusion
  33.6 0.7 scatter_custom_fusion
  34.3 0.7 all_to_all.22
  35.0 1.2 multiply_multiply_fusion.2
  36.2 4.0 fusion.28
  40.2 4.3 %negate_convert_fusion = (bf16[1,512,512]{1,2,0:T(8,128)(2,1)S(1)}, bf16[1,512,512]{1,2,0:T(8,128)(2,1)S(1)}) fusion(), kind=kLoop, calls=%fused_computation.31 | loop fusion | flops 4456448 | bytes 1048576 | tf_op jit(solution)/shard_map/slice | solution.py:22
  44.6 1.2 maximum_bitcast_fusion.2
  45.8 0.1 broadcast_add_fusion
  45.9 0.1 broadcast_add_fusion.1
  46.0 39.6 %all-to-all-done.1 = bf16[2,32,256,128]{2,1,0,3:T(8,128)(2,1)} async-done(((bf16[2,32,256,128]{2,1,0,3:T(8,128)(2,1)}), bf16[2,32,256,128]{2,1,0,3:T(8,128)(2,1)}, u32[]{:S(2)}, u32[]{:S(2)}) %all-to-all-start.1) | async-done | bytes 4194336 | tf_op jit(solution)/shard_map/all_to_all | solution.py:98
  85.5 10.3 %all-to-all-start = ((f32[16,1,2]{2,1,0:T(1,128)}), f32[16,1,2]{2,1,0:T(1,128)S(1)}, u32[]{:S(2)}, u32[]{:S(2)}) async-start(f32[16,1,2]{2,1,0:T(1,128)} %bitcast.7), calls=%async_computation | async-start | bytes 16384 | tf_op jit(solution)/shard_map/all_to_all | solution.py:151
  95.8 0.0 copy-start.3
  95.8 2.9 copy.32
  98.8 0.0 copy-done.3
  98.8 4.5 %convolution_bitcast_fusion = f32[2,8,512,256]{3,2,1,0:T(8,128)S(1)} fusion(bf16[2,512,256,8,1]{2,1,0,3,4:T(8,128)(2,1)S(1)} %bitcast.113, bf16[1,2,512,512]{2,3,1,0:T(8,128)(2,1)S(1)} %copy-done.3, bf16[1,2,512,512]{2,3,1,0:T(8,128)(2,1)S(1)} %get-tuple-element.16), kind=kOutput, calls=%fused_computation.17 | convolution fusion | flops 4299161600 | bytes 14680064 | tf_op jit(solution)/shard_map/qabc,pqae->pceb/dot_general | solution.py:96
  103.3 19.3 %multiply_add_fusion = (f32[1,8,512,256]{3,2,1,0:T(8,128)}, f32[1,8,512,256]{3,2,1,0:T(8,128)}) fusion(f32[2,8,512,256]{3,2,1,0:T(8,128)S(1)} %convolution_bitcast_fusion, f32[256]{0:T(256)S(1)} %get-tuple-element.38, f32[8,512]{1,0:T(8,128)S(1)} %broadcast_add_fusion, f32[256]{0:T(256)S(1)} %get-tuple-element.37, f32[8,512]{1,0:T(8,128)S(1)} %broadcast_add_fusion.1), kind=kLoop, calls=%fused_computation.10 | loop fusion | flops 13631488 | bytes 16812032 | tf_op jit(solution)/shard_map/add | solution.py:56
  122.6 8.1 %stack.67 = f32[1,8,8,64,4,64]{5,4,3,2,1,0:T(4,128)} reshape(f32[1,8,512,256]{3,2,1,0:T(8,128)} %get-tuple-element.15) | data formatting | bytes 8388608 | tf_op jit(solution)/shard_map/stack | solution.py:57
  130.7 7.6 %constant_dynamic-update-slice_fusion.1 = f32[2,8,8,64,4,64]{5,4,3,2,1,0:T(4,128)} fusion(f32[1,8,8,64,4,64]{5,4,3,2,1,0:T(4,128)} %stack.67), kind=kLoop, calls=%fused_computation.76 | loop fusion | bytes 12582912
  138.3 8.1 %stack.68 = f32[1,8,8,64,4,64]{5,4,3,2,1,0:T(4,128)} reshape(f32[1,8,512,256]{3,2,1,0:T(8,128)} %get-tuple-element.14) | data formatting | bytes 8388608 | tf_op jit(solution)/shard_map/stack | solution.py:57
  146.4 7.6 %constant_dynamic-update-slice_fusion = f32[2,8,8,64,4,64]{5,4,3,2,1,0:T(4,128)} fusion(f32[2,8,8,64,4,64]{5,4,3,2,1,0:T(4,128)} %constant_dynamic-update-slice_fusion.1, f32[1,8,8,64,4,64]{5,4,3,2,1,0:T(4,128)} %stack.68), kind=kLoop, calls=%fused_computation.75 | loop fusion | bytes 16777216 | tf_op jit(solution)/shard_map/stack | solution.py:57
  154.0 34.0 %conditional.1 = (f32[32,2,8,4096]{3,2,1,0:T(8,128)}) conditional(s32[]{:T(128)} %convert_element_type.135, f32[8,4,2,8,64,64]{5,1,4,0,3,2:T(4,128)} %bitcast.108, f32[2,8,8,64,4,64]{5,4,3,2,1,0:T(4,128)} %constant_dynamic-update-slice_fusion), branch_computations={%region_2.3_spmd, %region_3.4_spmd} | conditional | bytes 33554440 | solution.py:121
  154.0 19.2 %copy.27 = f32[8,4,2,8,64,64]{5,4,3,2,1,0:T(8,128)} copy(f32[8,4,2,8,64,64]{4,1,5,0,3,2:T(4,128)} %bitcast.109) | data formatting | bytes 16777216 | tf_op jit(solution)/shard_map/cond/branch_1_fun/transpose;transpose | solution.py:71
  173.2 14.8 %reshape.528 = f32[32,2,8,4096]{3,2,1,0:T(8,128)} reshape(f32[8,4,2,8,64,64]{5,4,3,2,1,0:T(8,128)} %copy.27) | data formatting | bytes 16777216 | tf_op jit(solution)/shard_map/reshape | solution.py:123
  188.0 7.7 %broadcast_multiply_fusion = f32[32,2,8,4096]{3,2,1,0:T(8,128)} fusion(f32[32,2,8,4096]{3,2,1,0:T(8,128)} %get-tuple-element.39, f32[]{:T(128)} %bitcast.43), kind=kLoop, calls=%fused_computation.9 | loop fusion | flops 2097152 | bytes 16777220 | tf_op jit(solution)/shard_map/mul | solution.py:126
  195.7 4.3 broadcast_in_dim.5
  200.0 15.4 %scatter_fusion = f32[32,2,8,4096]{3,2,1,0:T(8,128)} fusion(f32[32,2,8,4096]{3,2,1,0:T(8,128)} %broadcast_in_dim.5, s32[32]{0:T(128)S(1)} %fusion.53, f32[32,2,8,4096]{3,2,1,0:T(8,128)} %broadcast_multiply_fusion), kind=kCustom, calls=%fused_computation.2 | custom fusion | bytes 25165952 | tf_op jit(solution)/shard_map/scatter | solution.py:140
  215.3 0.0 all-to-all-done
  215.3 7.0 %all-to-all-start.2 = ((f32[16,2,2,8,4096]{4,3,2,1,0:T(8,128)}), f32[16,2,2,8,4096]{4,3,2,1,0:T(8,128)}, u32[]{:S(2)}, u32[]{:S(2)}) async-start(f32[16,2,2,8,4096]{4,3,2,1,0:T(8,128)} %bitcast.110), calls=%async_computation.2 | async-start | bytes 16777216 | tf_op jit(solution)/shard_map/all_to_all | solution.py:150
  222.3 0.5 broadcast.694
  222.8 0.7 reduce.3
  223.5 0.1 eq.39
  223.6 182.2 %all-to-all-done.2 = f32[16,2,2,8,4096]{4,3,2,1,0:T(8,128)} async-done(((f32[16,2,2,8,4096]{4,3,2,1,0:T(8,128)}), f32[16,2,2,8,4096]{4,3,2,1,0:T(8,128)}, u32[]{:S(2)}, u32[]{:S(2)}) %all-to-all-start.2) | async-done | bytes 8388640 | tf_op jit(solution)/shard_map/all_to_all | solution.py:150
  405.9 7.4 %reshape.532 = f32[32,65536]{1,0:T(8,128)} reshape(f32[16,2,2,8,4096]{4,3,2,1,0:T(8,128)} %all-to-all-done.2) | data formatting | bytes 16777216 | tf_op jit(solution)/shard_map/reshape | solution.py:158
  413.3 8.2 %copy.45 = f32[4,8,16,4096]{3,2,1,0:T(8,128)S(1)} copy(f32[4,8,16,4096]{3,1,2,0:T(8,128)} %bitcast.112) | data formatting | bytes 16777216
  421.5 0.0 copy-start.1
  421.6 7.7 %fusion = f32[3,2,8,4096]{3,0,2,1:T(4,128)S(1)} fusion(f32[2,8,4096,32]{2,1,0,3:T(8,128)S(1)} %bitcast.111, f32[32]{0:T(128)S(1)} %eq.39, f32[3]{0:T(128)S(1)} %iota_convert_fusion), kind=kOutput, calls=%fused_computation.4 | convolution fusion | flops 75497568 | bytes 9175180 | tf_op jit(solution)/shard_map/dot_general | solution.py:157
  429.3 1.3 copy.35
  430.6 0.0 copy-done.1
  (11 shorter events, 0.1 us)
Async XLA Ops:
  0.0 2.4 copy-start
  15.4 7.8 %copy-start.6 = (s32[1,3]{1,0:T(1,128)S(1)}, s32[1,3]{1,0:T(1,128)}, u32[]{:S(2)}) copy-start(s32[1,3]{1,0:T(1,128)} %param.10) | copy-start | bytes 40
  15.4 9.7 %copy-start.4 = (f32[3]{0:T(128)S(1)}, f32[3]{0:T(128)}, u32[]{:S(2)}) copy-start(f32[3]{0:T(128)} %param.14) | copy-start | bytes 40
  15.4 12.7 %copy-start.5 = (f32[3]{0:T(128)S(1)}, f32[3]{0:T(128)}, u32[]{:S(2)}) copy-start(f32[3]{0:T(128)} %param.15) | copy-start | bytes 40
  15.4 17.3 %copy-start.2 = (s32[64]{0:T(128)S(1)}, s32[64]{0:T(128)}, u32[]{:S(2)}) copy-start(s32[64]{0:T(128)} %param.13) | copy-start | bytes 772
  15.4 70.1 %all-to-all-start.1 = ((bf16[2,32,256,128]{2,1,0,3:T(8,128)(2,1)}), bf16[2,32,256,128]{2,1,0,3:T(8,128)(2,1)}, u32[]{:S(2)}, u32[]{:S(2)}) async-start(bf16[2,32,256,128]{2,1,0,3:T(8,128)(2,1)} %copy.30), calls=%async_computation.1 | async-start | bytes 8388608 | tf_op jit(solution)/shard_map/all_to_all | solution.py:98
  85.5 129.8 %all-to-all-start = ((f32[16,1,2]{2,1,0:T(1,128)}), f32[16,1,2]{2,1,0:T(1,128)S(1)}, u32[]{:S(2)}, u32[]{:S(2)}) async-start(f32[16,1,2]{2,1,0:T(1,128)} %bitcast.7), calls=%async_computation | async-start | bytes 16384 | tf_op jit(solution)/shard_map/all_to_all | solution.py:151
  95.8 2.9 copy-start.3
  215.3 190.5 %all-to-all-start.2 = ((f32[16,2,2,8,4096]{4,3,2,1,0:T(8,128)}), f32[16,2,2,8,4096]{4,3,2,1,0:T(8,128)}, u32[]{:S(2)}, u32[]{:S(2)}) async-start(f32[16,2,2,8,4096]{4,3,2,1,0:T(8,128)} %bitcast.110), calls=%async_computation.2 | async-start | bytes 16777216 | tf_op jit(solution)/shard_map/all_to_all | solution.py:150
  421.5 9.1 %copy-start.1 = (bf16[1,32,256,128]{3,2,1,0:T(8,128)(2,1)S(1)}, bf16[1,32,256,128]{3,2,1,0:T(8,128)(2,1)}, u32[]{:S(2)}) copy-start(bf16[1,32,256,128]{3,2,1,0:T(8,128)(2,1)} %param.9) | copy-start | bytes 6291460
where the time goes:
time: 432 us; the launch traced here: 431 us
  waiting for transfers between devices  222 us (51%)
  local copies, waits for them, and re-layouts  117 us (27%)
  other arithmetic  41.3 us (10%)
  starting transfers between devices  25.1 us (6%)
  matrix products  17.2 us (4%)
  between operations  7.74 us (2%)
    all_to_all x1, waiting for transfers between devices, body(): lax.all_to_all(outgoing, 'grid', split_axis=0, concat_axis=0, tiled=True)  182 us
    all_to_all x1, waiting for transfers between devices, body(): lax.all_to_all(along_mid, 'pencil', split_axis=3, concat_axis=1, tiled=True)  39.6 us
    another operation x3, local copies, waits for them, and re-layouts, apply_factor(): return jnp.stack([real_part, imag_part])  23.8 us
    add x1, other arithmetic, apply_factor(): imag_part = spectrum[0] * factor_im + spectrum[1] * factor_re  19.3 us
    another operation x1, local copies, waits for them, and re-layouts, turn_inner(): return grouped.transpose(0, 1, 2, 3, 5, 4)  19.2 us
    unnamed x16, local copies, waits for them, and re-layouts  15.9 us
    scatter x1, local copies, waits for them, and re-layouts, body(): outgoing = jnp.zeros_like(weighted).at[target].set(weighted).reshape(grid...  15.4 us
    reshape x1, local copies, waits for them, and re-layouts, body(): blocks = turned.reshape(held_count, 2, z_local, block_len * block_len)  14.8 us
  transfers between devices with their start and end apart: 3, of which 2 were waited for; matrix products, arithmetic and copies ran while one was open for 31% of the time, Pallas kernels for 0%

commit v1 on v0

v1 whole, which is shorter than its diff:
```python
import functools
import math

import jax
import jax.numpy as jnp
import ml_dtypes
import numpy as np
from jax import lax
from jax.sharding import PartitionSpec as P

BF16 = ml_dtypes.bfloat16


def dft_table(length):
    positions = np.arange(length, dtype=np.int64)
    angles = (positions[:, None] * positions[None, :] % length) * (2.0 * math.pi / length)
    return np.cos(angles).astype(BF16).astype(np.float32), (-np.sin(angles)).astype(BF16).astype(np.float32)


def slot_positions(g):
    return [2 * g, 32 if g == 0 else 64 - 2 * g, 2 * g + 1, 63 - 2 * g]


@functools.cache
def mid_table():
    cos, sin = dft_table(256)
    rows = np.zeros((16, 2, 4, 2, 256), np.float32)
    for g in range(16):
        for grp in range(2):
            for i, n in enumerate(slot_positions(g)):
                m = n + 64 * grp
                rows[g, grp, i, 0] = cos[m]
                rows[g, grp, i, 1] = sin[m]
    rows[0, 0, 0, 1] = cos[128]
    return rows.reshape(256, 256).astype(BF16)


@functools.cache
def z_tables():
    cos, sin = dft_table(128)
    c = cos.reshape(16, 8, 128).transpose(2, 0, 1)
    s = sin.reshape(16, 8, 128).transpose(2, 0, 1)
    e = (c, s)
    ie = (-s, c)
    out = np.zeros((3, 2, 2, 128, 16, 2, 2, 2, 8), np.float32)

    def put(variant, i2, ab, sign, slot, pair, scale):
        for q in range(2):
            out[variant, i2, ab, :, :, sign, slot, q, :] = scale * pair[q]

    for variant in range(3):
        for i2 in range(2):
            if variant == 1 and i2 == 0:
                put(1, 0, 0, 0, 0, e, 1.0)
                put(1, 0, 1, 1, 0, e, 1.0)
                continue
            back = 1 - i2 if variant == 0 else i2
            put(variant, i2, 0, 0, i2, e, 1.0)
            put(variant, i2, 1, 0, i2, ie, 1.0)
            put(variant, i2, 0, 1, back, e, 1.0)
            put(variant, i2, 1, 1, back, ie, -1.0)
    return out.reshape(3, 512, 1024).astype(BF16)


@functools.cache
def long_table():
    cos, sin = dft_table(512)
    return np.concatenate([cos, sin], axis=1).astype(BF16)


def owner_codes(owner_map):
    ids = jnp.arange(64, dtype=jnp.int32)
    bx, by = ids // 8, ids % 8
    in_x, in_y = (bx >= 2) & (bx < 6), (by >= 2) & (by < 6)
    kind = jnp.where(in_x, 1, jnp.where(in_y, 2, 0))
    key = jnp.where(owner_map >= 0, (owner_map // 3) * 3 + kind, -1)
    match = key[None, :] == jnp.arange(48, dtype=jnp.int32)[:, None]
    return jnp.sum(jnp.where(match, (ids * 4 + owner_map % 3)[None, :], 0), axis=1)


def body(field, levels, coefficients, failed, owner_map, velocity, diffusivity):
    g = lax.axis_index("grid")
    p = lax.axis_index("pencil")
    kind = (levels[0, 0] < levels[0, 1]).astype(jnp.int32)
    weight = (coefficients[0] * (1 - failed[0])).astype(jnp.float32)
    v = jnp.einsum("rm,amz->arz", jnp.asarray(mid_table()), field[0], preferred_element_type=jnp.float32)
    v = (v * weight).astype(jnp.bfloat16)
    zero = jnp.zeros_like(v)
    both = jnp.stack([jnp.where(kind == 0, v, zero), jnp.where(kind == 1, v, zero)])
    both = both.reshape(2, 32, 16, 16, 128)
    s = lax.psum_scatter(both, "grid", scatter_dimension=2, tiled=False)
    s = s.reshape(2, 32, 2, 2, 512)
    w = jnp.asarray(z_tables())
    first = g == 0
    wa = jnp.where(first, w[1], w[0])
    wb = jnp.where(first, w[2], w[0])
    f32 = jnp.float32
    u0a = jnp.einsum("kaz,zn->kan", s[:, :, 0, 0], wa, preferred_element_type=f32)
    u0b = jnp.einsum("kaz,zn->kan", s[:, :, 1, 0], wb, preferred_element_type=f32)
    u1 = jnp.einsum("kacz,zn->kacn", s[:, :, :, 1], w[0], preferred_element_type=f32)
    lane = jnp.arange(1024) % 64
    swap = first & (lane >= 32) & (lane < 48)
    u0 = jnp.stack([jnp.where(swap, u0b, u0a), jnp.where(swap, u0a, u0b)], axis=2)
    u = jnp.stack([u0, u1], axis=3).astype(jnp.bfloat16)
    chunk = u.reshape(2, 32, 2, 2, 16, 64).transpose(4, 0, 2, 1, 3, 5).reshape(16, 4, 32, 128)
    r = lax.all_to_all(chunk, "pencil", split_axis=0, concat_axis=0, tiled=True)
    table = jnp.asarray(long_table()).reshape(16, 32, 1024)
    res = jnp.einsum("pkal,pan->kln", r, table, preferred_element_type=f32)
    res = res.reshape(2, 2, 2, 2, 2, 2, 8, 2, 512)
    re = res[:, :, :, :, :, 0, :, 0] - res[:, :, :, :, :, 1, :, 1]
    im = res[:, :, :, :, :, 1, :, 0] + res[:, :, :, :, :, 0, :, 1]
    longs = jnp.arange(512, dtype=jnp.int32)
    k_long = jnp.where(longs < 256, longs, longs - 512).astype(f32)
    n0 = jnp.array([0, 64, 1, 63]) + g * jnp.array([2, -2, 2, -2])
    n = jnp.where((g == 0) & (jnp.arange(4) == 1), 32, n0).reshape(2, 2)
    base = jnp.array([[0, -64], [64, -128]])
    k_mid = (n[None, :, None, :] + base[:, None, :, None]).astype(f32)
    zs = p * 8 + jnp.arange(8, dtype=jnp.int32)
    k_z = jnp.where(zs < 64, zs, zs - 128).astype(f32)
    shape = (2, 2, 2, 2, 2, 8, 512)
    kl = jnp.broadcast_to(k_long, shape)
    km = jnp.broadcast_to(k_mid[None, :, :, :, :, None, None], shape)
    kz = jnp.broadcast_to(k_z[:, None], shape)
    is0 = (jnp.arange(2) == 0).reshape(2, 1, 1, 1, 1, 1, 1)
    kx, ky = jnp.where(is0, kl, km), jnp.where(is0, km, kl)
    expo = (diffusivity[0] * kx * kx + diffusivity[1] * ky * ky + diffusivity[2] * kz * kz) * (-4.0 / 512**2)
    phase = (velocity[0] * kx + velocity[1] * ky + velocity[2] * kz) * (-2.0 * math.pi / 256)
    mag = jnp.exp(expo) * (1.0 / 4096)
    fr, fi = mag * jnp.cos(phase), mag * jnp.sin(phase)
    f = jnp.stack([re * fr - im * fi, re * fi + im * fr], axis=5).astype(jnp.bfloat16)
    f = f.reshape(2, 2, 2, 2, 2, 2, 8, 8, 64).transpose(0, 1, 3, 7, 2, 4, 5, 6, 8).reshape(2, 32, 4, 2, 8, 64)
    codes = owner_codes(owner_map).reshape(16, 3)
    blk = codes // 4
    bx, by = blk // 8, blk % 8

    def index(lb, gb):
        sign = gb // 4
        grp = (gb % 2) ^ sign
        return (grp * 2 + sign) * 8 + lb

    i0 = index(bx[:, :2], by[:, :2])
    i1 = index(jnp.stack([by[:, 0], by[:, 2]], 1), jnp.stack([bx[:, 0], bx[:, 2]], 1))
    out = jnp.stack([f[0][i0], f[1][i1]], axis=1)
    rb = lax.all_to_all(out, "grid", split_axis=0, concat_axis=0, tiled=True)
    order = np.zeros(64, np.int32)
    for gg in range(16):
        for i, nn in enumerate(slot_positions(gg)):
            order[nn] = gg * 4 + i
    rb = rb.astype(f32).transpose(1, 2, 4, 5, 0, 3, 6).reshape(2, 2, 2, 8, 64, 64)[:, :, :, :, order]
    k0 = rb[0].transpose(0, 1, 2, 4, 3)
    k1 = rb[1]
    classes = jnp.stack([k0[0] + k1[0], k0[1], k1[1]]).reshape(3, 2, 8, 4096)
    slots = codes[g] % 4
    which = jnp.sum(jnp.where(slots[None, :] == jnp.arange(3)[:, None], jnp.arange(3)[None, :], 0), axis=1)
    return classes[which]


def solution(mesh):
    placed = (P("grid", "pencil", None, None), P("grid", None), P("grid"), P("grid"), P(), P(), P())
    return jax.shard_map(
        body, mesh=mesh, in_specs=placed, out_specs=P("grid", None, "pencil", None), check_vma=False
    )
```

time: 432 us -> 189 us (0.44)
  waiting for transfers between devices: 222 us -> 82.9 us
  local copies, waits for them, and re-layouts: 117 us -> 42.7 us
  other arithmetic: 41.3 us -> 21.2 us
  matrix products: 17.2 us -> 8.12 us
  between operations: 7.74 us -> 16.4 us
  starting transfers between devices: 25.1 us -> 17 us
    all_to_all x3 -> x2, waiting for transfers between devices: 222 us -> 25.8 us  [the longest x1 17.3 us: body(): rb = lax.all_to_all(out, 'grid', split_axis=0, concat_axis=0, tiled=True)]
    reduce_scatter x0 -> x1, waiting for transfers between devices: none -> 57.1 us  [body(): s = lax.psum_scatter(both, 'grid', scatter_dimension=2, tiled=False)]
    another operation x4 -> x9, local copies, waits for them, and re-layouts: 43 us -> 8.96 us  [the longest x3 3.34 us: body(): classes = jnp.stack([k0[0] + k1[0], k0[1], k1[1]]).reshape(3, 2, 8, 4096)]
    reshape x2, local copies, waits for them, and re-layouts: 22.2 us -> 1.37 us  [the longest x1 1.29 us: body(): u.reshape(2, 32, 2, 2, 16, 64).transpose(4, 0, 2, 1, 3, 5)]
    add x4 -> x1, other arithmetic: 19.5 us -> 1.96 us  [body(): classes = jnp.stack([k0[0] + k1[0], k0[1], k1[1]]).reshape(3, 2, 8, 4096)]
    scatter x2 -> x0, local copies, waits for them, and re-layouts: 16 us -> none  [the longest x1 15.4 us: body(): outgoing = jnp.zeros_like(weighted).at[target].set(weighted).reshape(grid...]
    unnamed x16 -> x39, local copies, waits for them, and re-layouts: 15.9 us -> 6.5 us
    dot_general x3 -> x5, matrix products: 17.2 us -> 8.12 us  [the longest x1 3.14 us: body(): res = jnp.einsum('pkal,pan->kln', r, table, preferred_element_type=f32)]
  transfers between devices with their start and end apart: 3 -> 3, of which waited for: 2 -> 3; matrix products, arithmetic and copies ran while one was open for 31% -> 3% of each run, Pallas kernels for 0% -> 0%
where the time goes in v1:
time: 189 us; the launch traced here: 188 us
  waiting for transfers between devices  82.9 us (44%)
  local copies, waits for them, and re-layouts  42.7 us (23%)
  other arithmetic  21.2 us (11%)
  starting transfers between devices  17 us (9%)
  between operations  16.4 us (9%)
  matrix products  8.12 us (4%)
    reduce_scatter x1, waiting for transfers between devices, body(): s = lax.psum_scatter(both, 'grid', scatter_dimension=2, tiled=False)  57.1 us
    all_to_all x1, waiting for transfers between devices, body(): rb = lax.all_to_all(out, 'grid', split_axis=0, concat_axis=0, tiled=True)  17.3 us
    all_to_all x1, starting transfers between devices, body(): rb = lax.all_to_all(out, 'grid', split_axis=0, concat_axis=0, tiled=True)  10.4 us
    another operation x1, other arithmetic  8.57 us
    all_to_all x1, waiting for transfers between devices, body(): r = lax.all_to_all(chunk, 'pencil', split_axis=0, concat_axis=0, tiled=True)  8.5 us
    all_to_all x1, starting transfers between devices, body(): r = lax.all_to_all(chunk, 'pencil', split_axis=0, concat_axis=0, tiled=True)  6.61 us
    unnamed x39, local copies, waits for them, and re-layouts  6.5 us
  transfers between devices with their start and end apart: 3, of which 3 were waited for; matrix products, arithmetic and copies ran while one was open for 3% of the time, Pallas kernels for 0%

profile of v1, /device:TPU:1, one launch (start us, length us, event | category | flops | bytes accessed | tf_op | source)
XLA Modules:
  0.0 188.3 jit_solution(14945384084151040940)
XLA Ops:
  6.5 1.4 fusion.61
  10.6 1.6 broadcast_select_fusion.1
  12.2 0.4 pad_maximum_fusion
  12.6 3.1 %copy.109 = bf16[2,32,16,16,128]{4,3,1,0,2:T(8,128)(2,1)} copy(bf16[2,32,16,16,128]{4,3,2,1,0:T(8,128)(2,1)S(1)} %pad_maximum_fusion) | data formatting | bytes 8388608 | tf_op jit(solution)/shard_map/stack | solution.py:89
  15.8 0.6 copy-done.15
  16.4 0.1 select_reduce_fusion
  16.5 0.1 reshape.486
  16.6 0.6 fusion.48
  17.2 0.6 fusion.59
  17.9 0.7 fusion.60
  18.5 1.8 multiply_multiply_fusion
  20.3 0.2 slice_reduce_fusion.1
  20.6 0.6 compare_select_fusion.2
  21.1 0.6 fusion.42
  21.7 0.5 and_select_fusion.9
  22.2 57.1 %reduce-scatter.2.cloned.1.call-done = bf16[2,32,1,16,128]{4,3,1,0,2:T(8,128)(2,1)} async-done(((bf16[2,32,16,16,128]{4,3,1,0,2:T(8,128)(2,1)}), bf16[2,32,1,16,128]{4,3,1,0,2:T(8,128)(2,1)}) %reduce-scatter.2.cloned.1.call-update) | async-done | bytes 262160 | tf_op jit(solution)/shard_map/reduce_scatter | solution.py:91
  79.3 1.1 reshape_reduce_scatter.3
  80.4 0.2 fusion.58
  80.6 1.0 slice.143
  81.6 0.3 fusion.19
  82.0 1.0 select_convert_fusion.1
  83.0 1.1 stack.64
  84.2 0.2 stack.65
  84.4 2.0 %fusion.6 = bf16[2,32,2,1,16,64]{5,1,4,2,0,3:T(8,128)(2,1)S(1)} fusion(bf16[16,64,512,1,1]{2,1,0,4,3:T(8,128)(2,1)} %constant.227, bf16[2,32,2,1,512]{4,3,2,1,0:T(2,128)(2,1)} %slice.143), kind=kOutput, calls=%fused_computation.19 | convolution fusion | flops 134348800 | bytes 1441792 | tf_op jit(solution)/shard_map/kacz,zn->kacn/dot_general | solution.py:100
  86.4 0.3 maximum_bitcast_fusion
  86.7 1.1 copy.89
  87.8 1.3 reshape.484
  89.1 6.6 %all-to-all-start = ((bf16[16,4,32,128]{3,2,1,0:T(8,128)(2,1)}), bf16[16,4,32,128]{3,2,1,0:T(8,128)(2,1)S(1)}, u32[]{:S(2)}, u32[]{:S(2)}) async-start(bf16[16,4,32,128]{3,2,1,0:T(8,128)(2,1)} %reshape.484), calls=%async_computation.1 | async-start | bytes 1048576 | tf_op jit(solution)/shard_map/all_to_all | solution.py:106
  95.7 0.1 add.261
  95.8 0.1 reshape.494
  95.9 0.1 copy.96
  96.0 0.1 reshape.502
  96.1 0.1 add_convert_fusion.1
  96.2 8.5 %all-to-all-done = bf16[16,4,32,128]{3,2,1,0:T(8,128)(2,1)S(1)} async-done(((bf16[16,4,32,128]{3,2,1,0:T(8,128)(2,1)}), bf16[16,4,32,128]{3,2,1,0:T(8,128)(2,1)S(1)}, u32[]{:S(2)}, u32[]{:S(2)}) %all-to-all-start) | async-done | bytes 524320 | tf_op jit(solution)/shard_map/all_to_all | solution.py:106
  104.7 2.5 %copy.90 = bf16[4,128,32,16]{2,3,1,0:T(8,128)(2,1)} copy(bf16[4,128,32,16]{1,2,0,3:T(8,128)(2,1)S(1)} %bitcast.123) | data formatting | bytes 1048576 | tf_op jit(solution)/shard_map/pkal,pan->kln/dot_general | solution.py:108
  107.2 3.1 %fusion.3 = f32[2,2,2,2,2,2,8,2,512]{8,6,7,5,4,3,2,1,0:T(8,128)S(1)} fusion(bf16[2,512,32,16,1,1,1,1,1,1]{1,2,3,0,9,8,7,6,5,4:T(8,128)(2,1)} %constant.228, bf16[2,2,2,2,2,2,8,32,16,1]{7,8,6,5,4,3,2,1,0,9:T(8,128)(2,1)} %bitcast.122), kind=kOutput, calls=%fused_computation.17 | convolution fusion | flops 536870912 | bytes 3670016 | tf_op jit(solution)/shard_map/pkal,pan->kln/dot_general | solution.py:108
  110.3 1.2 slice_subtract_fusion
  111.5 1.2 add.272
  112.8 2.2 %sub.75 = f32[2,2,2,2,2,1,8,8,64]{8,7,6,4,3,2,1,0,5:T(8,128)} reshape(f32[2,2,2,2,2,1,8,1,512]{8,6,7,5,4,3,2,1,0:T(8,128)} %get-tuple-element.11) | data formatting | bytes 1048576 | tf_op jit(solution)/shard_map/sub | solution.py:110
  115.0 8.6 %subtract_convert_fusion = (bf16[2,2,2,2,2,1,8,8,64]{8,6,5,4,2,7,3,1,0:T(8,128)(2,1)S(1)}, bf16[2,2,2,2,2,1,8,8,64]{8,6,5,4,2,7,3,1,0:T(8,128)(2,1)S(1)}) fusion(f32[2,2,2,2,2,1,8,8,64]{8,7,6,4,3,2,1,0,5:T(8,128)S(1)} %add.272, f32[2,2,2,2,2,1,8,8,64]{8,7,6,4,3,2,1,0,5:T(8,128)} %sub.75, f32[8]{0:T(128)S(1)} %copy-done.9, f32[]{:T(128)} %bitcast.33, ...), kind=kLoop, calls=%fused_computation.41 | loop fusion | flops 3276800 | bytes 1575058 | tf_op jit(solution)/shard_map/convert.2
  123.6 0.2 maximum_bitcast_fusion.1
  123.8 0.1 fusion.57
  124.0 1.4 gather_fusion
  125.4 1.4 gather_fusion.1
  126.8 1.5 copy_bitcast_fusion.6
  128.3 1.5 reshape.542
  129.9 10.4 %all-to-all-start.1 = ((bf16[16,2,8192]{2,1,0:T(2,128)(2,1)}), bf16[16,2,8192]{2,1,0:T(2,128)(2,1)}, u32[]{:S(2)}, u32[]{:S(2)}) async-start(bf16[16,2,8192]{2,1,0:T(2,128)(2,1)} %reshape.542), calls=%async_computation.2 | async-start | bytes 1048576 | tf_op jit(solution)/shard_map/all_to_all | solution.py:144
  140.3 0.1 select_reduce_fusion.1
  140.4 17.3 %all-to-all-done.1 = bf16[16,2,8192]{2,1,0:T(2,128)(2,1)} async-done(((bf16[16,2,8192]{2,1,0:T(2,128)(2,1)}), bf16[16,2,8192]{2,1,0:T(2,128)(2,1)}, u32[]{:S(2)}, u32[]{:S(2)}) %all-to-all-start.1) | async-done | bytes 524320 | tf_op jit(solution)/shard_map/all_to_all | solution.py:144
  157.7 2.3 %reshape.543 = bf16[16,2,2,2,4,8,64]{6,5,4,3,2,1,0:T(8,128)(2,1)S(1)} reshape(bf16[16,2,8192]{2,1,0:T(2,128)(2,1)} %all-to-all-done.1) | data formatting | bytes 1048576
  160.0 1.6 copy_convert_fusion
  161.6 3.7 %gather_fusion.2 = f32[64,2,2,2,8,64]{5,4,3,2,1,0:T(8,128)} fusion(f32[2,2,2,8,64,64]{5,3,4,2,1,0:T(8,128)} %bitcast.120, s32[1024]{0:T(1024)S(1)} %pad_clamp_fusion.1), kind=kCustom, calls=%fused_computation.2 | custom fusion | bytes 2097408 | tf_op jit(solution)/shard_map/gather | solution.py:149
  165.3 2.3 %slice.156 = f32[1,2,2,8,64,64]{5,3,2,1,0,4:T(8,128)} slice(f32[2,2,2,8,64,64]{5,3,2,1,0,4:T(8,128)} %bitcast.117), slice={[0:1], [0:2], [0:2], [0:8], [0:64], [0:64]} | slice | bytes 1048576 | tf_op jit(solution)/shard_map/slice | solution.py:150
  167.6 1.9 slice.160
  169.5 2.0 %copy.116 = f32[1,2,2,8,64,64]{4,3,2,5,1,0:T(8,128)S(1)} copy(f32[1,2,2,8,64,64]{5,3,2,1,0,4:T(8,128)} %slice.156) | data formatting | bytes 1048576
  171.5 2.0 %fusion.27 = (f32[1,2,8,64,64]{4,2,1,3,0:T(8,128)S(1)}, f32[1,2,8,64,64]{4,2,1,3,0:T(8,128)}) fusion(f32[2,2,2,8,64,64]{5,3,2,1,0,4:T(8,128)} %bitcast.119, f32[2,2,8,64,64]{4,2,1,3,0:T(8,128)S(1)} %bitcast.121), kind=kLoop, calls=%fused_computation.48 | loop fusion | flops 65536 | bytes 1310720 | tf_op jit(solution)/shard_map/add | solution.py:152
  173.5 1.0 copy.101
  174.4 1.2 stack.78
  175.7 1.0 copy.102
  176.6 1.9 %stack.79 = f32[1,2,8,4096]{3,2,1,0:T(8,128)} reshape(f32[1,2,8,64,64]{4,3,2,1,0:T(8,128)} %copy.102) | data formatting | bytes 524288 | tf_op jit(solution)/shard_map/stack | solution.py:152
  178.6 0.2 copy.103
  178.7 0.2 stack.80
  178.9 1.0 pad_maximum_fusion.2
  179.9 1.5 gather_fusion.3
  (49 shorter events, 0.3 us)
Async XLA Ops:
  6.5 4.1 %copy-start = (bf16[1,32,256,128]{3,2,1,0:T(8,128)(2,1)S(1)}, bf16[1,32,256,128]{3,2,1,0:T(8,128)(2,1)}, u32[]{:S(2)}) copy-start(bf16[1,32,256,128]{3,2,1,0:T(8,128)(2,1)} %param.15) | copy-start | bytes 6291460
  6.5 72.8 %reduce-scatter.2.cloned.1.call-start = ((), (), s32[]{:S(2)}) async-start(), calls=%async_computation.3 | async-start | bytes 4456448 | tf_op jit(solution)/shard_map/reduce_scatter | solution.py:91
  15.8 0.7 copy-start.15
  15.8 1.5 copy-start.5
  15.8 2.1 %copy-start.6 = (f32[3]{0:T(128)S(1)}, f32[3]{0:T(128)}, u32[]{:S(2)}) copy-start(f32[3]{0:T(128)} %param.20) | copy-start | bytes 40
  15.8 6.0 %copy-start.12 = (s32[4]{0:T(128)S(1)}, s32[4]{0:T(128)}, u32[]{:S(2)}) copy-start(s32[4]{0:T(128)} %constant.206.clone) | copy-start | bytes 52
  15.8 6.0 %copy-start.13 = (s32[4]{0:T(128)S(1)}, s32[4]{0:T(128)}, u32[]{:S(2)}) copy-start(s32[4]{0:T(128)} %constant.207.clone) | copy-start | bytes 52
  15.8 65.8 %copy-start.3 = (bf16[1,512,1024]{2,1,0:T(8,128)(2,1)S(1)}, bf16[1,512,1024]{2,1,0:T(8,128)(2,1)}, u32[]{:S(2)}) copy-start(bf16[1,512,1024]{2,1,0:T(8,128)(2,1)} %constant.216) | copy-start | bytes 3145732
  80.4 1.5 copy-start.16
  80.4 1.5 copy-start.17
  86.7 9.0 %copy-start.14 = (s32[4]{0:T(128)S(1)}, s32[4]{0:T(128)}, u32[]{:S(2)}) copy-start(s32[4]{0:T(128)} %and_select_fusion.9) | copy-start | bytes 52
  86.7 9.2 %copy-start.7 = (s32[16,2,1]{0,2,1:T(1,128)S(1)}, s32[16,2,1]{0,2,1:T(1,128)}, u32[]{:S(2)}) copy-start(s32[16,2,1]{0,2,1:T(1,128)} %compare_select_fusion.2) | copy-start | bytes 388
  86.7 9.4 %copy-start.10 = (s32[2,2]{1,0:T(2,128)S(1)}, s32[2,2]{1,0:T(2,128)}, u32[]{:S(2)}) copy-start(s32[2,2]{1,0:T(2,128)} %constant.208.clone) | copy-start | bytes 52
  89.1 15.6 %all-to-all-start = ((bf16[16,4,32,128]{3,2,1,0:T(8,128)(2,1)}), bf16[16,4,32,128]{3,2,1,0:T(8,128)(2,1)S(1)}, u32[]{:S(2)}, u32[]{:S(2)}) async-start(bf16[16,4,32,128]{3,2,1,0:T(8,128)(2,1)} %reshape.484), calls=%async_computation.1 | async-start | bytes 1048576 | tf_op jit(solution)/shard_map/all_to_all | solution.py:106
  111.5 3.5 %copy-start.4 = (f32[8,64]{1,0:T(8,128)S(1)}, f32[8,64]{1,0:T(8,128)}, u32[]{:S(2)}) copy-start(f32[8,64]{1,0:T(8,128)} %fusion.42) | copy-start | bytes 6148
  111.5 3.5 %copy-start.8 = (f32[8]{0:T(128)S(1)}, f32[8]{0:T(128)}, u32[]{:S(2)}) copy-start(f32[8]{0:T(128)} %get-tuple-element.35) | copy-start | bytes 100
  111.5 3.5 %copy-start.9 = (f32[8]{0:T(128)S(1)}, f32[8]{0:T(128)}, u32[]{:S(2)}) copy-start(f32[8]{0:T(128)} %get-tuple-element.36) | copy-start | bytes 100
  126.8 13.4 %copy-start.11 = (s32[64]{0:T(128)S(1)}, s32[64]{0:T(128)}, u32[]{:S(2)}) copy-start(s32[64]{0:T(128)} %constant.225) | copy-start | bytes 772
  129.9 27.8 %all-to-all-start.1 = ((bf16[16,2,8192]{2,1,0:T(2,128)(2,1)}), bf16[16,2,8192]{2,1,0:T(2,128)(2,1)}, u32[]{:S(2)}, u32[]{:S(2)}) async-start(bf16[16,2,8192]{2,1,0:T(2,128)(2,1)} %reshape.542), calls=%async_computation.2 | async-start | bytes 1048576 | tf_op jit(solution)/shard_map/all_to_all | solution.py:144
  173.5 2.2 %copy-start.1 = (f32[1,2,8,64,64]{4,2,1,3,0:T(8,128)S(1)}, f32[1,2,8,64,64]{4,2,1,3,0:T(8,128)}, u32[]{:S(2)}) copy-start(f32[1,2,8,64,64]{4,2,1,3,0:T(8,128)} %get-tuple-element.16) | copy-start | bytes 786436
  173.5 5.1 %copy-start.2 = (f32[1,1,2,8,64,64]{5,3,2,1,0,4:T(8,128)S(1)}, f32[1,1,2,8,64,64]{5,3,2,1,0,4:T(8,128)}, u32[]{:S(2)}) copy-start(f32[1,1,2,8,64,64]{5,3,2,1,0,4:T(8,128)} %slice.160) | copy-start | bytes 786436
Sparse Core Ops, SparseCore 0:
  15.9 63.3 reduce-scatter.1

commit v2 on v1

v2 whole, which is shorter than its diff:
```python
import functools
import math

import jax
import jax.numpy as jnp
import ml_dtypes
import numpy as np
from jax import lax
from jax.experimental import pallas as pl
from jax.experimental.pallas import tpu as pltpu
from jax.sharding import PartitionSpec as P

BF16 = ml_dtypes.bfloat16
F32 = jnp.float32
MESH = pl.DeviceIdType.MESH


def dft_table(length):
    positions = np.arange(length, dtype=np.int64)
    angles = (positions[:, None] * positions[None, :] % length) * (2.0 * math.pi / length)
    return np.cos(angles).astype(BF16).astype(np.float32), (-np.sin(angles)).astype(BF16).astype(np.float32)


def slot_positions(g):
    return [2 * g, 32 if g == 0 else 64 - 2 * g, 2 * g + 1, 63 - 2 * g]


@functools.cache
def mid_table():
    cos, sin = dft_table(256)
    rows = np.zeros((16, 2, 4, 2, 256), np.float32)
    for g in range(16):
        for grp in range(2):
            for i, n in enumerate(slot_positions(g)):
                rows[g, grp, i, 0] = cos[n + 64 * grp]
                rows[g, grp, i, 1] = sin[n + 64 * grp]
    rows[0, 0, 0, 1] = cos[128]
    return rows.reshape(256, 256).astype(BF16)


@functools.cache
def z_bases():
    cos, sin = dft_table(128)
    c = cos.reshape(16, 8, 128).transpose(2, 0, 1)
    s = sin.reshape(16, 8, 128).transpose(2, 0, 1)
    both = np.stack([np.stack([c, s], 2), np.stack([-s, c], 2)])
    full = np.broadcast_to(both[:, :, :, None], (2, 128, 16, 4, 2, 8))
    return full.reshape(2, 128, 1024).astype(BF16)


@functools.cache
def z_masks():
    out = np.zeros((3, 2, 2, 2, 16, 2, 2, 16), np.float32)

    def put(variant, i2, ab, sign, slot, which, scale):
        out[variant, i2, ab, which, :, sign, slot] = scale

    for variant in range(3):
        for i2 in range(2):
            if variant == 1 and i2 == 0:
                put(1, 0, 0, 0, 0, 0, 1.0)
                put(1, 0, 1, 1, 0, 0, 1.0)
                continue
            back = 1 - i2 if variant == 0 else i2
            put(variant, i2, 0, 0, i2, 0, 1.0)
            put(variant, i2, 1, 0, i2, 1, 1.0)
            put(variant, i2, 0, 1, back, 0, 1.0)
            put(variant, i2, 1, 1, back, 1, -1.0)
    return out.reshape(24, 1, 1024)


@functools.cache
def long_table():
    cos, sin = dft_table(512)
    return np.concatenate([cos, sin], axis=1).astype(BF16)


@functools.cache
def order_table():
    out = np.zeros((64, 128), np.float32)
    for g in range(16):
        for i, n in enumerate(slot_positions(g)):
            out[g * 4 + i, n] = 1.0
            out[g * 4 + i, n + 64] = 1.0
    return out.astype(BF16)


def owner_codes(owner_map):
    ids = jnp.arange(64, dtype=jnp.int32)
    bx, by = ids // 8, ids % 8
    in_x, in_y = (bx >= 2) & (bx < 6), (by >= 2) & (by < 6)
    kind = jnp.where(in_x, 1, jnp.where(in_y, 2, 0))
    key = jnp.where(owner_map >= 0, (owner_map // 3) * 3 + kind, -1)
    match = key[None, :] == jnp.arange(48, dtype=jnp.int32)[:, None]
    return jnp.sum(jnp.where(match, (ids * 4 + owner_map % 3)[None, :], 0), axis=1, dtype=jnp.int32)


PLUS_D = (4, 3, 3, 2, 2, 1, 1)
PLUS_H = (0, 1, 0, 1, 0, 1, 0)


def transform_kernel(
    levels, coefficients, failed, codes, velocity, diffusivity, field, mid_tab, base_tab, masks, long_tab,
    landing,
    fbuf, tbuf, ebuf, tlbuf, wbuf, v, xr, xk, sb, rz, sf, lhs0, lhs1, chunk, rows, ff, sb2, flong, frow,
    load_sem, xs_sem, xr_sem, zs_sem, zr_sem, ps_sem, pr_sem, gs_sem, gr_sem,
):
    g = lax.axis_index("grid")
    p = lax.axis_index("pencil")
    zc, core = g // 2, g % 2
    py, px = p // 4, p % 4

    loads = [
        pltpu.make_async_copy(mid_tab, tbuf, load_sem.at[0]),
        pltpu.make_async_copy(field.at[0, pl.ds(0, 16)], fbuf.at[pl.ds(0, 16)], load_sem.at[1]),
        pltpu.make_async_copy(field.at[0, pl.ds(16, 16)], fbuf.at[pl.ds(16, 16)], load_sem.at[2]),
        pltpu.make_async_copy(base_tab, ebuf, load_sem.at[3]),
        pltpu.make_async_copy(long_tab, tlbuf, load_sem.at[4]),
    ]
    for load in loads:
        load.start()

    barrier = pltpu.get_barrier_semaphore()
    for s in range(1, 16):
        og = 2 * lax.rem(zc + s // 2, 8) + lax.rem(core + s % 2, 2)
        pl.semaphore_signal(barrier, inc=1, device_id=(og, p), device_id_type=MESH)
        op = 4 * lax.rem(py + s // 4, 4) + lax.rem(px + s % 4, 4)
        pl.semaphore_signal(barrier, inc=1, device_id=(g, op), device_id_type=MESH)

    kind = jnp.where(levels[0, 0] < levels[0, 1], 1.0, 0.0).astype(F32)
    weight = (coefficients[0] * (1 - failed[0])).astype(F32)
    loads[0].wait()

    def mid_step(k, carry):
        pair = jnp.concatenate([fbuf[2 * k], fbuf[2 * k + 1]], axis=1)
        y = jnp.dot(tbuf[...], pair, preferred_element_type=F32) * weight
        yb = y.astype(jnp.bfloat16)
        v[:, pl.ds(2 * k, 1)] = yb[:, :128].reshape(16, 1, 16, 128)
        v[:, pl.ds(2 * k + 1, 1)] = yb[:, 128:].reshape(16, 1, 16, 128)
        return carry

    loads[1].wait()
    lax.fori_loop(0, 8, mid_step, 0)
    loads[2].wait()
    lax.fori_loop(8, 16, mid_step, 0)

    xk[0] = jnp.full((16, 128), kind, F32)
    pl.semaphore_wait(barrier, 30)

    mate = (g + 1 - 2 * core, p)
    kind_copy = pltpu.make_async_remote_copy(
        xk.at[0], xk.at[1], xs_sem.at[16], xr_sem.at[16], device_id=mate, device_id_type=MESH
    )
    kind_copy.start()
    swaps = {}
    order = [(4, 0), (4, 1), (3, 1), (5, 0), (3, 0), (5, 1), (2, 1), (6, 0), (2, 0), (6, 1)]
    order += [(1, 1), (7, 0), (1, 0), (7, 1), (0, 0), (0, 1)]
    for d, h in order:
        z = lax.rem(zc + d, 8)
        swaps[d, h] = pltpu.make_async_remote_copy(
            v.at[2 * z + 1 - core, pl.ds(16 * h, 16)],
            xr.at[z, pl.ds(16 * h, 16)],
            xs_sem.at[2 * d + h],
            xr_sem.at[2 * d + h],
            device_id=mate,
            device_id_type=MESH,
        )
        swaps[d, h].start()
    kind_copy.wait_recv()
    other = xk[1][None]
    mine = kind

    def own_sum(z, at, k):
        me = v[2 * z + core, pl.ds(at, 4)].astype(F32)
        mate_part = xr[z, pl.ds(at, 4)].astype(F32)
        if k == 0:
            return me * (1.0 - mine) + mate_part * (1.0 - other)
        return me * mine + mate_part * other

    hops = {}
    for n in range(7):
        for way in range(2):
            d = PLUS_D[n] if way == 0 else 8 - PLUS_D[n]
            h = PLUS_H[n] if way == 0 else 1 - PLUS_H[n]
            z = lax.rem(zc + d, 8)
            swaps[d, h].wait_recv()
            if n >= 2:
                hops[way, n - 2].wait_recv()

            def add_step(a, carry, n=n, way=way, h=h, z=z):
                for k in range(2):
                    total = own_sum(z, 16 * h + 4 * a, k)
                    if n >= 2:
                        total = total + rz[way, n - 2, k, pl.ds(4 * a, 4)].astype(F32)
                    sb[way, n, k, pl.ds(4 * a, 4)] = total.astype(jnp.bfloat16)
                return carry

            lax.fori_loop(0, 4, add_step, 0)
            to = lax.rem(zc + (1 if way == 0 else 7), 8)
            hops[way, n] = pltpu.make_async_remote_copy(
                sb.at[way, n],
                rz.at[way, n],
                zs_sem.at[way, n],
                zr_sem.at[way, n],
                device_id=(2 * to + core, p),
                device_id_type=MESH,
            )
            hops[way, n].start()

    loads[3].wait()
    first = jnp.where(g == 0, 1, 0)
    for variant in range(3):
        var = variant * first
        for blk in range(4):

            def table_step(c, carry, variant=variant, blk=blk, var=var):
                at = pl.ds(16 * c, 16)
                me = masks[8 * var + 2 * blk]
                mi = masks[8 * var + 2 * blk + 1]
                val = ebuf[0, at].astype(F32) * me + ebuf[1, at].astype(F32) * mi
                wbuf[variant, pl.ds(128 * blk + 16 * c, 16)] = val.astype(jnp.bfloat16)
                return carry

            lax.fori_loop(0, 8, table_step, 0)

    lanes = lax.broadcasted_iota(jnp.int32, (8, 512), 1)
    k_long = jnp.where(lanes < 256, lanes, lanes - 512).astype(F32)
    for k in range(2):
        mag = jnp.exp(diffusivity[k] * k_long * k_long * (-4.0 / 512**2))
        ph = velocity[k] * k_long * (-2.0 * math.pi / 256)
        flong[k, 0] = mag * jnp.cos(ph)
        flong[k, 1] = mag * jnp.sin(ph)

    def row_step(k, carry):
        r = lax.broadcasted_iota(jnp.int32, (128, 128), 0)
        i2, sign = (r >> 3) & 1, (r >> 4) & 1
        pair, grp = (r >> 5) & 1, (r >> 6) & 1
        pos = jnp.where(i2 == 0, 2 * g + pair, jnp.where((pair == 0) & (g == 0), 32, 64 - 2 * g - pair))
        base = jnp.where(grp == 0, -64 * sign, 64 - 192 * sign)
        k_mid = (pos + base).astype(F32)
        zi = 8 * p + (r & 7)
        k_z = jnp.where(zi < 64, zi, zi - 128).astype(F32)
        d_mid = diffusivity[1 - k]
        v_mid = velocity[1 - k]
        mag = jnp.exp((d_mid * k_mid * k_mid + diffusivity[2] * k_z * k_z) * (-4.0 / 512**2)) * (1.0 / 4096)
        ph = (v_mid * k_mid + velocity[2] * k_z) * (-2.0 * math.pi / 256)
        frow[k, 0] = mag * jnp.cos(ph)
        frow[k, 1] = mag * jnp.sin(ph)
        return carry

    for k in range(2):
        row_step(k, 0)

    for h in range(2):
        swaps[0, h].wait_recv()
        a_way, b_way = (6, 5) if h == 0 else (5, 6)
        hops[0, a_way].wait_recv()
        hops[1, b_way].wait_recv()

        def last_step(a, carry, h=h, a_way=a_way, b_way=b_way):
            for k in range(2):
                total = own_sum(zc, 16 * h + 4 * a, k)
                total = total + rz[0, a_way, k, pl.ds(4 * a, 4)].astype(F32)
                total = total + rz[1, b_way, k, pl.ds(4 * a, 4)].astype(F32)
                sf[k, pl.ds(256 * h + 64 * a, 64)] = total.reshape(64, 128)
            return carry

        lax.fori_loop(0, 4, last_step, 0)

    for k in range(2):
        for grp in range(2):
            for pair in range(2):
                for e in range(4):
                    j = grp * 8 + pair * 4 + e
                    part = sf[k, pl.ds(j, 32, stride=16)].astype(jnp.bfloat16)
                    if pair == 0:
                        lhs0[grp, pl.ds(32 * k, 32), pl.ds(128 * e, 128)] = part
                    else:
                        lhs1[pl.ds(64 * k + 32 * grp, 32), pl.ds(128 * e, 128)] = part
    lane64 = lax.broadcasted_iota(jnp.int32, (64, 128), 1)
    l64 = lane64 % 64
    low = lane64 < 64
    swap = (l64 >= 32) & (l64 < 48) & (g == 0)
    low32 = low[:32]
    for t in range(8):
        cols = pl.ds(128 * t, 128)
        ua = jnp.dot(lhs0[0], wbuf[1, :, cols], preferred_element_type=F32)
        ub = jnp.dot(lhs0[1], wbuf[2, :, cols], preferred_element_type=F32)
        u1 = jnp.dot(lhs1[...], wbuf[0, :, cols], preferred_element_type=F32)
        u0 = (jnp.where(swap, ub, ua), jnp.where(swap, ua, ub))
        u0r = (pltpu.roll(u0[0], 64, 1), pltpu.roll(u0[1], 64, 1))
        u1r = pltpu.roll(u1, 64, 1)
        for k in range(2):
            for grp in range(2):
                at = slice(64 * k + 32 * grp, 64 * k + 32 * grp + 32)
                a0, a0r = u0[grp][32 * k : 32 * k + 32], u0r[grp][32 * k : 32 * k + 32]
                chunk[2 * t, 2 * k + grp] = jnp.where(low32, a0, u1r[at]).astype(jnp.bfloat16)
                chunk[2 * t + 1, 2 * k + grp] = jnp.where(low32, a0r, u1[at]).astype(jnp.bfloat16)

    outs = []
    for s in (10, 11, 14, 9, 6, 15, 13, 7, 5, 8, 2, 12, 4, 3, 1):
        op = 4 * lax.rem(py + s // 4, 4) + lax.rem(px + s % 4, 4)
        copy = pltpu.make_async_remote_copy(
            chunk.at[op], rows.at[p], ps_sem.at[s], pr_sem.at[s], device_id=(g, op), device_id_type=MESH
        )
        copy.start()
        outs.append(copy)
    rows[pl.ds(p, 1)] = chunk[pl.ds(p, 1)]
    loads[4].wait()
    for copy in outs:
        copy.wait_recv()

    for kg in range(4):
        k = kg // 2
        line = rows[:, kg].reshape(512, 128)
        turned = line.T
        for t in range(4):
            col_c = tlbuf[:, pl.ds(128 * t, 128)]
            col_s = tlbuf[:, pl.ds(512 + 128 * t, 128)]
            both = jnp.dot(turned, jnp.concatenate([col_c, col_s], axis=1), preferred_element_type=F32)
            c = both[:, :128].reshape(8, 2, 8, 128)
            sn = both[:, 128:].reshape(8, 2, 8, 128)
            re = c[:, 0] - sn[:, 1]
            im = c[:, 1] + sn[:, 0]
            rr = frow[k, 0, pl.ds(64 * (kg % 2), 64)].reshape(8, 8, 128)
            ri = frow[k, 1, pl.ds(64 * (kg % 2), 64)].reshape(8, 8, 128)
            lr = flong[k, 0, :, pl.ds(128 * t, 128)][None]
            li = flong[k, 1, :, pl.ds(128 * t, 128)][None]
            er = rr * lr - ri * li
            ei = rr * li + ri * lr
            out_re = re * er - im * ei
            out_im = re * ei + im * er
            full = jnp.stack([out_re, out_im], axis=1).reshape(2, 2, 2, 16, 128)
            spun = pltpu.roll(full.reshape(128, 128), 64, 1).reshape(2, 2, 2, 16, 128)
            for sign in range(2):
                at = ((kg * 2 + 0) * 4 + t) * 2 + sign
                ff[at] = full[:, sign].reshape(64, 128).astype(jnp.bfloat16)
                ff[at + 8] = spun[:, sign].reshape(64, 128).astype(jnp.bfloat16)

    def piece(k, lb, gb, high):
        sign = gb >> 2
        grp = (gb & 1) ^ sign
        rot = (lb & 1) if high == 0 else 1 - (lb & 1)
        at = (((2 * k + grp) * 2 + rot) * 4 + (lb >> 1)) * 2 + sign
        return ff[at].astype(F32)

    finals = []
    for s in (8, 9, 7, 6, 10, 11, 5, 4, 12, 13, 3, 2, 14, 15, 1, 0):
        og = 2 * lax.rem(zc + s // 2, 8) + lax.rem(core + s % 2, 2)
        ca, cb, cc = (codes[3 * og + c] >> 2 for c in range(3))
        ax, ay = ca >> 3, ca & 7
        bx, by = cb >> 3, cb & 7
        cx, cy = cc >> 3, cc & 7
        sb2[s, 0] = jnp.where(low, piece(0, ax, ay, 0), piece(0, bx, by, 1)).astype(jnp.bfloat16)
        sb2[s, 1] = jnp.where(low, piece(1, ay, ax, 0), piece(1, cy, cx, 1)).astype(jnp.bfloat16)
        if s:
            copy = pltpu.make_async_remote_copy(
                sb2.at[s], landing.at[g], gs_sem.at[s], gr_sem.at[s], device_id=(og, p), device_id_type=MESH
            )
            copy.start()
            finals.append(copy)
        else:
            own = pltpu.make_async_copy(sb2.at[0], landing.at[g], gs_sem.at[0])
            own.start()
    own.wait()
    for copy in finals:
        copy.wait()
    for copy in outs:
        copy.wait_send()
    for copy in hops.values():
        copy.wait_send()
    for copy in swaps.values():
        copy.wait_send()
    kind_copy.wait_send()


def place_kernel(codes, landed, order, out, f0, d0, k0):
    g = lax.axis_index("grid")
    slot = [codes[3 * g + c] & 3 for c in range(3)]
    for gg in range(16):
        f0[pl.ds(64 * gg, 64)] = landed[gg, 0].astype(F32)
    low32 = lax.broadcasted_iota(jnp.int32, (32, 128), 1) < 64
    low8 = low32[:8]
    for q in range(2):
        for z in range(8):
            rows = f0[pl.ds(8 * q + z, 64, stride=16)].astype(jnp.bfloat16)
            buf = z % 2
            d0[buf] = jnp.dot(rows.T, order[...], preferred_element_type=F32)
            for c in range(2):
                even = d0[buf, pl.ds(64 * c, 32, stride=2)]
                odd = d0[buf, pl.ds(64 * c + 1, 32, stride=2)]
                k0[c, q, pl.ds(z, 32, stride=8)] = jnp.where(low32, even, odd)
    for x2 in range(32):
        ge, ie = (x2, 0) if x2 < 16 else ((0, 1) if x2 == 16 else (32 - x2, 1))
        go, io = (x2, 2) if x2 < 16 else (31 - x2, 3)
        even = landed[ge, 1, pl.ds(16 * ie, 16)].astype(F32)
        odd = landed[go, 1, pl.ds(16 * io, 16)].astype(F32)
        for q in range(2):
            e, o = even[8 * q : 8 * q + 8], odd[8 * q : 8 * q + 8]
            first = jnp.where(low8, e, pltpu.roll(o, 64, 1))
            third = jnp.where(low8, pltpu.roll(e, 64, 1), o)
            at = pl.ds(8 * x2, 8)
            cols = pl.ds(128 * x2, 128)
            out[slot[0], q, :, cols] = first + k0[0, q, at]
            out[slot[1], q, :, cols] = k0[1, q, at]
            out[slot[2], q, :, cols] = third


def body(field, levels, coefficients, failed, owner_map, velocity, diffusivity):
    codes = owner_codes(owner_map)
    smem = pl.BlockSpec(memory_space=pltpu.SMEM)
    vmem = pl.BlockSpec(memory_space=pltpu.VMEM)
    anyspace = pl.BlockSpec(memory_space=pl.ANY)
    bf = jnp.bfloat16
    dma = pltpu.SemaphoreType.DMA
    landed = pl.pallas_call(
        transform_kernel,
        out_shape=jax.ShapeDtypeStruct((16, 2, 64, 128), bf),
        in_specs=[smem] * 6 + [anyspace] * 3 + [vmem] + [anyspace],
        out_specs=anyspace,
        scratch_shapes=[
            pltpu.VMEM((32, 256, 128), bf),
            pltpu.VMEM((256, 256), bf),
            pltpu.VMEM((2, 128, 1024), bf),
            pltpu.VMEM((512, 1024), bf),
            pltpu.VMEM((3, 512, 1024), bf),
            pltpu.VMEM((16, 32, 16, 128), bf),
            pltpu.VMEM((8, 32, 16, 128), bf),
            pltpu.VMEM((2, 16, 128), F32),
            pltpu.VMEM((2, 7, 2, 16, 16, 128), bf),
            pltpu.VMEM((2, 7, 2, 16, 16, 128), bf),
            pltpu.VMEM((2, 512, 128), F32),
            pltpu.VMEM((2, 64, 512), bf),
            pltpu.VMEM((128, 512), bf),
            pltpu.VMEM((16, 4, 32, 128), bf),
            pltpu.VMEM((16, 4, 32, 128), bf),
            pltpu.VMEM((64, 64, 128), bf),
            pltpu.VMEM((16, 2, 64, 128), bf),
            pltpu.VMEM((2, 2, 8, 512), F32),
            pltpu.VMEM((2, 2, 128, 128), F32),
            dma((5,)), dma((17,)), dma((17,)), dma((2, 7)), dma((2, 7)),
            dma((16,)), dma((16,)), dma((16,)), dma((16,)),
        ],
        compiler_params=pltpu.CompilerParams(
            collective_id=0, has_side_effects=True, vmem_limit_bytes=56 * 2**20
        ),
        name="transform",
    )(
        levels, coefficients, failed, codes, velocity, diffusivity, field,
        jnp.asarray(mid_table()), jnp.asarray(z_bases()), jnp.asarray(z_masks()), jnp.asarray(long_table()),
    )
    return pl.pallas_call(
        place_kernel,
        out_shape=jax.ShapeDtypeStruct((3, 2, 8, 4096), F32),
        in_specs=[smem, vmem, vmem],
        out_specs=vmem,
        scratch_shapes=[
            pltpu.VMEM((1024, 128), F32),
            pltpu.VMEM((2, 128, 128), F32),
            pltpu.VMEM((2, 2, 256, 128), F32),
        ],
        compiler_params=pltpu.CompilerParams(vmem_limit_bytes=32 * 2**20),
        name="place",
    )(codes, landed, jnp.asarray(order_table()))


def solution(mesh):
    placed = (P("grid", "pencil", None, None), P("grid", None), P("grid"), P("grid"), P(), P(), P())
    return jax.shard_map(
        body, mesh=mesh, in_specs=placed, out_specs=P("grid", None, "pencil", None), check_vma=False
    )
```

time: 189 us -> 66.9 us (0.35)
  waiting for transfers between devices: 82.9 us -> 0 us
  Pallas kernels: 0 us -> 63 us
  local copies, waits for them, and re-layouts: 42.7 us -> 1.04 us
  other arithmetic: 21.2 us -> 1.3 us
  starting transfers between devices: 17 us -> 0 us
  between operations: 16.4 us -> 1.33 us
  matrix products: 8.12 us -> 0 us
    pallas_call x0 -> x2, Pallas kernels: none -> 63 us  [the longest x1 61.1 us: body(): pl.pallas_call(transform_kernel, out_shape=jax.ShapeDtypeStruct((16, 2, 6...]
    reduce_scatter x1 -> x0, waiting for transfers between devices: 57.1 us -> none  [body(): s = lax.psum_scatter(both, 'grid', scatter_dimension=2, tiled=False)]
    all_to_all x2 -> x0, waiting for transfers between devices: 25.8 us -> none  [the longest x1 17.3 us: body(): rb = lax.all_to_all(out, 'grid', split_axis=0, concat_axis=0, tiled=True)]
    all_to_all x2 -> x0, starting transfers between devices: 17 us -> none  [the longest x1 10.4 us: body(): rb = lax.all_to_all(out, 'grid', split_axis=0, concat_axis=0, tiled=True)]
    another operation x3 -> x0, other arithmetic: 9.95 us -> none
    slice x11 -> x0, local copies, waits for them, and re-layouts: 9.51 us -> none  [the longest x3 3.02 us: body(): classes = jnp.stack([k0[0] + k1[0], k0[1], k1[1]]).reshape(3, 2, 8, 4096)]
    another operation x9 -> x0, local copies, waits for them, and re-layouts: 8.96 us -> none  [the longest x3 3.34 us: body(): classes = jnp.stack([k0[0] + k1[0], k0[1], k1[1]]).reshape(3, 2, 8, 4096)]
    dot_general x5 -> x0, matrix products: 8.12 us -> none  [the longest x1 3.14 us: body(): res = jnp.einsum('pkal,pan->kln', r, table, preferred_element_type=f32)]
  transfers between devices with their start and end apart: 3 -> 0, of which waited for: 3 -> 0; matrix products, arithmetic and copies ran while one was open for 3% -> 0% of each run, Pallas kernels for 0% -> 0%
where the time goes in v2:
time: 66.9 us; the launch traced here: 66.7 us
  Pallas kernels  63 us (94%)
  between operations  1.33 us (2%)
  other arithmetic  1.3 us (2%)
  local copies, waits for them, and re-layouts  1.04 us (2%)
    pallas_call x1, Pallas kernels, body(): pl.pallas_call(transform_kernel, out_shape=jax.ShapeDtypeStruct((16, 2, 6...  61.1 us
    pallas_call x1, Pallas kernels, body(): pl.pallas_call(place_kernel, out_shape=jax.ShapeDtypeStruct((3, 2, 8, 409...  1.95 us

profile of v2, /device:TPU:1, one launch (start us, length us, event | category | flops | bytes accessed | tf_op | source)
XLA Modules:
  0.0 66.7 jit_solution(6532054510146504513)
XLA Ops:
  1.3 0.7 %compare_select_fusion = (s32[64]{0:T(128)S(1)}, s32[64]{0:T(128)S(1)}) fusion(s32[64]{0:T(128)} %param.16), kind=kLoop, calls=%fused_computation.8 | loop fusion | flops 2432 | bytes 768 | tf_op jit(solution)/shard_map/jit(_where)/select_n | solution.py:93
  2.0 0.6 select_reduce_fusion.codes
  2.6 0.0 copy-start.1
  2.6 0.0 copy-start.2
  2.6 61.1 %transform.1.landed = bf16[16,2,64,128]{3,2,1,0:T(8,128)(2,1)} custom-call(s32[1,3]{1,0:T(1,128)} %levels.1, s32[1]{0:T(128)S(6)} %copy.13.coefficients, s32[1]{0:T(128)S(6)} %copy.14.failed, s32[48]{0:T(128)} %select_reduce_fusion.codes, f32[3]{0:T(128)} %velocity.1, f32[3]{0:T(128)} %diffusivity.1, bf16[1,32,256,128]{3,2,1,0:T(8,128)(2,1)} %field.1, ...), custom_call_target="tpu_custom_call" | custom-call | tf_op jit(solution)/shard_map/transform/pallas_call | solution.py:416
  63.7 0.0 copy-done.1
  63.7 0.0 copy-done.2
  63.7 0.0 copy-start
  63.7 1.0 %copy-done = bf16[16,2,64,128]{3,2,1,0:T(8,128)(2,1)S(1)} copy-done((bf16[16,2,64,128]{3,2,1,0:T(8,128)(2,1)S(1)}, bf16[16,2,64,128]{3,2,1,0:T(8,128)(2,1)}, u32[]{:S(2)}) %copy-start) | copy-done | bytes 524312
  64.7 2.0 %place.1 = f32[3,2,8,4096]{3,2,1,0:T(8,128)} custom-call(s32[48]{0:T(128)S(1)} %copy-done.2, bf16[16,2,64,128]{3,2,1,0:T(8,128)(2,1)S(1)} %copy-done, bf16[64,128]{1,0:T(8,128)(2,1)S(1)} %copy-done.1), custom_call_target="tpu_custom_call" | custom-call | tf_op jit(solution)/shard_map/place/pallas_call | solution.py:452
Async XLA Ops:
  2.6 61.1 %copy-start.1 = (bf16[64,128]{1,0:T(8,128)(2,1)S(1)}, bf16[64,128]{1,0:T(8,128)(2,1)}, u32[]{:S(2)}) copy-start(bf16[64,128]{1,0:T(8,128)(2,1)} %constant.68.clone.order) | copy-start | bytes 49156
  2.6 61.1 %copy-start.2 = (s32[48]{0:T(128)S(1)}, s32[48]{0:T(128)}, u32[]{:S(2)}) copy-start(s32[48]{0:T(128)} %select_reduce_fusion.codes) | copy-start | bytes 580
  63.7 1.0 %copy-start = (bf16[16,2,64,128]{3,2,1,0:T(8,128)(2,1)S(1)}, bf16[16,2,64,128]{3,2,1,0:T(8,128)(2,1)}, u32[]{:S(2)}) copy-start(bf16[16,2,64,128]{3,2,1,0:T(8,128)(2,1)} %transform.1.landed) | copy-start | bytes 1572868

commit v3 on v2

v3 whole, which is shorter than its diff:
```python
import functools
import math

import jax
import jax.numpy as jnp
import ml_dtypes
import numpy as np
from jax import lax
from jax.experimental import pallas as pl
from jax.experimental.pallas import tpu as pltpu
from jax.sharding import PartitionSpec as P

BF16 = ml_dtypes.bfloat16
F32 = jnp.float32
MESH = pl.DeviceIdType.MESH


def dft_table(length):
    positions = np.arange(length, dtype=np.int64)
    angles = (positions[:, None] * positions[None, :] % length) * (2.0 * math.pi / length)
    return np.cos(angles).astype(BF16).astype(np.float32), (-np.sin(angles)).astype(BF16).astype(np.float32)


def slot_positions(g):
    return [2 * g, 32 if g == 0 else 64 - 2 * g, 2 * g + 1, 63 - 2 * g]


@functools.cache
def mid_table():
    cos, sin = dft_table(256)
    rows = np.zeros((16, 2, 4, 2, 256), np.float32)
    for g in range(16):
        for grp in range(2):
            for i, n in enumerate(slot_positions(g)):
                rows[g, grp, i, 0] = cos[n + 64 * grp]
                rows[g, grp, i, 1] = sin[n + 64 * grp]
    rows[0, 0, 0, 1] = cos[128]
    return rows.reshape(256, 256).astype(BF16)


@functools.cache
def z_bases():
    cos, sin = dft_table(128)
    c = cos.reshape(16, 8, 128).transpose(2, 0, 1)
    s = sin.reshape(16, 8, 128).transpose(2, 0, 1)
    both = np.stack([np.stack([c, s], 2), np.stack([-s, c], 2)])
    full = np.broadcast_to(both[:, :, :, None], (2, 128, 16, 4, 2, 8))
    return full.reshape(2, 128, 1024).astype(BF16)


@functools.cache
def z_masks():
    out = np.zeros((3, 2, 2, 2, 16, 2, 2, 16), np.float32)

    def put(variant, i2, ab, sign, slot, which, scale):
        out[variant, i2, ab, which, :, sign, slot] = scale

    for variant in range(3):
        for i2 in range(2):
            if variant == 1 and i2 == 0:
                put(1, 0, 0, 0, 0, 0, 1.0)
                put(1, 0, 1, 1, 0, 0, 1.0)
                continue
            back = 1 - i2 if variant == 0 else i2
            put(variant, i2, 0, 0, i2, 0, 1.0)
            put(variant, i2, 1, 0, i2, 1, 1.0)
            put(variant, i2, 0, 1, back, 0, 1.0)
            put(variant, i2, 1, 1, back, 1, -1.0)
    return out.reshape(24, 1, 1024)


@functools.cache
def long_table():
    cos, sin = dft_table(512)
    return np.concatenate([cos, sin], axis=1).astype(BF16)


@functools.cache
def order_table():
    out = np.zeros((64, 128), np.float32)
    for g in range(16):
        for i, n in enumerate(slot_positions(g)):
            out[g * 4 + i, n] = 1.0
            out[g * 4 + i, n + 64] = 1.0
    return out.astype(BF16)


PLUS_D = (4, 3, 3, 2, 2, 1, 1)
PLUS_H = (0, 1, 0, 1, 0, 1, 0)
CLASSES = (
    tuple(8 * x + y for x in (0, 1, 6, 7) for y in (0, 1, 6, 7)),
    tuple(8 * x + y for x in (2, 3, 4, 5) for y in (0, 1, 6, 7)),
    tuple(8 * x + y for x in (0, 1, 6, 7) for y in (2, 3, 4, 5)),
)


def block_code(owner_map, owner, c):
    total = 0
    for b in CLASSES[c]:
        r = owner_map[b] - 3 * owner
        total = total + jnp.where((r >= 0) & (r < 3), 4 * b + r, 0)
    return total & 255


def transform_kernel(
    levels, coefficients, failed, owner_map, velocity, diffusivity, field, mid_tab, base_tab, mask_tab, long_tab,
    landing,
    fbuf, tbuf, ebuf, masks, tlbuf, wbuf, v, xr, xk, sb, rz, sf, lhs0, lhs1, chunk, rows, ff, sb2, flong, frow, codes,
    load_sem, xs_sem, xr_sem, zs_sem, zr_sem, ps_sem, pr_sem, gs_sem, gr_sem,
):
    g = lax.axis_index("grid")
    p = lax.axis_index("pencil")
    zc, core = g // 2, g % 2
    py, px = p // 4, p % 4

    loads = [
        pltpu.make_async_copy(mid_tab, tbuf, load_sem.at[0]),
        pltpu.make_async_copy(field.at[0, pl.ds(0, 16)], fbuf.at[pl.ds(0, 16)], load_sem.at[1]),
        pltpu.make_async_copy(field.at[0, pl.ds(16, 16)], fbuf.at[pl.ds(16, 16)], load_sem.at[2]),
        pltpu.make_async_copy(base_tab, ebuf, load_sem.at[3]),
        pltpu.make_async_copy(mask_tab, masks, load_sem.at[4]),
        pltpu.make_async_copy(long_tab, tlbuf, load_sem.at[5]),
    ]
    for load in loads:
        load.start()

    barrier = pltpu.get_barrier_semaphore()
    for s in (8, 9, 6, 7, 10, 11, 4, 5, 12, 13, 2, 3, 14, 15, 1):
        og = 2 * lax.rem(zc + s // 2, 8) + lax.rem(core + s % 2, 2)
        pl.semaphore_signal(barrier, inc=1, device_id=(og, p), device_id_type=MESH)
    for s in range(1, 16):
        op = 4 * lax.rem(py + s // 4, 4) + lax.rem(px + s % 4, 4)
        pl.semaphore_signal(barrier, inc=1, device_id=(g, op), device_id_type=MESH)

    kind = jnp.where(levels[0, 0] < levels[0, 1], 1.0, 0.0).astype(F32)
    weight = (coefficients[0] * (1 - failed[0])).astype(F32)
    loads[0].wait()

    def mid_step(k, carry):
        pair = jnp.concatenate([fbuf[2 * k], fbuf[2 * k + 1]], axis=1)
        y = jnp.dot(tbuf[...], pair, preferred_element_type=F32) * weight
        yb = y.astype(jnp.bfloat16)
        v[:, pl.ds(2 * k, 1)] = yb[:, :128].reshape(16, 1, 16, 128)
        v[:, pl.ds(2 * k + 1, 1)] = yb[:, 128:].reshape(16, 1, 16, 128)
        return carry

    loads[1].wait()
    lax.fori_loop(0, 8, mid_step, 0)
    loads[2].wait()
    lax.fori_loop(8, 16, mid_step, 0)

    def code_step(o, carry):
        for c in range(3):
            codes[3 * o + c] = block_code(owner_map, o, c)
        return carry

    lax.fori_loop(0, 16, code_step, 0)
    xk[0] = jnp.full((16, 128), kind, F32)
    pl.semaphore_wait(barrier, 30)

    mate = (g + 1 - 2 * core, p)
    kind_copy = pltpu.make_async_remote_copy(
        xk.at[0], xk.at[1], xs_sem.at[16], xr_sem.at[16], device_id=mate, device_id_type=MESH
    )
    kind_copy.start()
    swaps = {}
    order = [(4, 0), (4, 1), (3, 1), (5, 0), (3, 0), (5, 1), (2, 1), (6, 0), (2, 0), (6, 1)]
    order += [(1, 1), (7, 0), (1, 0), (7, 1), (0, 0), (0, 1)]
    for d, h in order:
        z = lax.rem(zc + d, 8)
        swaps[d, h] = pltpu.make_async_remote_copy(
            v.at[2 * z + 1 - core, pl.ds(16 * h, 16)],
            xr.at[z, pl.ds(16 * h, 16)],
            xs_sem.at[2 * d + h],
            xr_sem.at[2 * d + h],
            device_id=mate,
            device_id_type=MESH,
        )
        swaps[d, h].start()
    kind_copy.wait_recv()
    other = xk[1][None]
    mine = kind
    swapped = set()

    def await_swap(d, h):
        if (d, h) not in swapped:
            swapped.add((d, h))
            swaps[d, h].wait_recv()

    def own_sum(z, at, k):
        me = v[2 * z + core, pl.ds(at, 4)].astype(F32)
        mate_part = xr[z, pl.ds(at, 4)].astype(F32)
        if k == 0:
            return me * (1.0 - mine) + mate_part * (1.0 - other)
        return me * mine + mate_part * other

    hops = {}

    def hop(k, n):
        for way in range(2):
            d = PLUS_D[n] if way == 0 else 8 - PLUS_D[n]
            h = PLUS_H[n] if way == 0 else 1 - PLUS_H[n]
            z = lax.rem(zc + d, 8)
            await_swap(d, h)
            if n >= 2:
                hops[k, way, n - 2].wait_recv()

            def add_step(a, carry):
                total = own_sum(z, 16 * h + 4 * a, k)
                if n >= 2:
                    total = total + rz[k, way, n - 2, pl.ds(4 * a, 4)].astype(F32)
                sb[k, way, n, pl.ds(4 * a, 4)] = total.astype(jnp.bfloat16)
                return carry

            lax.fori_loop(0, 4, add_step, 0)
            to = lax.rem(zc + (1 if way == 0 else 7), 8)
            hops[k, way, n] = pltpu.make_async_remote_copy(
                sb.at[k, way, n],
                rz.at[k, way, n],
                zs_sem.at[k, way, n],
                zr_sem.at[k, way, n],
                device_id=(2 * to + core, p),
                device_id_type=MESH,
            )
            hops[k, way, n].start()

    def tables():
        loads[3].wait()
        loads[4].wait()
        first = jnp.where(g == 0, 1, 0)
        for variant in range(3):
            var = variant * first
            for blk in range(4):

                def table_step(c, carry):
                    at = pl.ds(16 * c, 16)
                    me = masks[8 * var + 2 * blk]
                    mi = masks[8 * var + 2 * blk + 1]
                    val = ebuf[0, at].astype(F32) * me + ebuf[1, at].astype(F32) * mi
                    wbuf[variant, pl.ds(128 * blk + 16 * c, 16)] = val.astype(jnp.bfloat16)
                    return carry

                lax.fori_loop(0, 8, table_step, 0)

    def factors():
        lanes = lax.broadcasted_iota(jnp.int32, (8, 512), 1)
        k_long = jnp.where(lanes < 256, lanes, lanes - 512).astype(F32)
        r = lax.broadcasted_iota(jnp.int32, (128, 128), 0)
        i2, sign = (r >> 3) & 1, (r >> 4) & 1
        pair, grp = (r >> 5) & 1, (r >> 6) & 1
        pos = jnp.where(i2 == 0, 2 * g + pair, jnp.where((pair == 0) & (g == 0), 32, 64 - 2 * g - pair))
        base = jnp.where(grp == 0, -64 * sign, 64 - 192 * sign)
        k_mid = (pos + base).astype(F32)
        zi = 8 * p + (r & 7)
        k_z = jnp.where(zi < 64, zi, zi - 128).astype(F32)
        for k in range(2):
            mag = jnp.exp(diffusivity[k] * k_long * k_long * (-4.0 / 512**2))
            ph = velocity[k] * k_long * (-2.0 * math.pi / 256)
            flong[k, 0] = mag * jnp.cos(ph)
            flong[k, 1] = mag * jnp.sin(ph)
            d_mid = diffusivity[1 - k]
            v_mid = velocity[1 - k]
            mag = jnp.exp((d_mid * k_mid * k_mid + diffusivity[2] * k_z * k_z) * (-4.0 / 512**2)) * (1.0 / 4096)
            ph = (v_mid * k_mid + velocity[2] * k_z) * (-2.0 * math.pi / 256)
            frow[k, 0] = mag * jnp.cos(ph)
            frow[k, 1] = mag * jnp.sin(ph)

    def collect(k):
        for h in range(2):
            await_swap(0, h)
            a_way, b_way = (6, 5) if h == 0 else (5, 6)
            hops[k, 0, a_way].wait_recv()
            hops[k, 1, b_way].wait_recv()

            def last_step(a, carry):
                total = own_sum(zc, 16 * h + 4 * a, k)
                total = total + rz[k, 0, a_way, pl.ds(4 * a, 4)].astype(F32)
                total = total + rz[k, 1, b_way, pl.ds(4 * a, 4)].astype(F32)
                sf[k, pl.ds(256 * h + 64 * a, 64)] = total.reshape(64, 128)
                return carry

            lax.fori_loop(0, 4, last_step, 0)

    lane = lax.broadcasted_iota(jnp.int32, (64, 128), 1)
    low = lane < 64
    low32 = low[:32]
    lane32 = lane[:32] % 64
    swap = (lane32 >= 32) & (lane32 < 48) & (g == 0)

    def along_z(k):
        for grp in range(2):
            for pair in range(2):
                for e in range(4):
                    j = grp * 8 + pair * 4 + e
                    part = sf[k, pl.ds(j, 32, stride=16)].astype(jnp.bfloat16)
                    if pair == 0:
                        lhs0[k, grp, :, pl.ds(128 * e, 128)] = part
                    else:
                        lhs1[k, pl.ds(32 * grp, 32), pl.ds(128 * e, 128)] = part
        for t2 in range(4):
            cols = pl.ds(256 * t2, 256)
            wide_a = jnp.dot(lhs0[k, 0], wbuf[1, :, cols], preferred_element_type=F32)
            wide_b = jnp.dot(lhs0[k, 1], wbuf[2, :, cols], preferred_element_type=F32)
            wide_1 = jnp.dot(lhs1[k], wbuf[0, :, cols], preferred_element_type=F32)
            for t1 in range(2):
                t = 2 * t2 + t1
                part = slice(128 * t1, 128 * t1 + 128)
                ua, ub, u1 = wide_a[:, part], wide_b[:, part], wide_1[:, part]
                u1r = pltpu.roll(u1, 64, 1)
                for grp in range(2):
                    u0 = jnp.where(swap, ub, ua) if grp == 0 else jnp.where(swap, ua, ub)
                    u0r = pltpu.roll(u0, 64, 1)
                    at = slice(32 * grp, 32 * grp + 32)
                    chunk[k, 2 * t, grp] = jnp.where(low32, u0, u1r[at]).astype(jnp.bfloat16)
                    chunk[k, 2 * t + 1, grp] = jnp.where(low32, u0r, u1[at]).astype(jnp.bfloat16)

    outs = {}

    def send_lines(k):
        for s in (10, 11, 14, 9, 6, 15, 13, 7, 5, 8, 2, 12, 4, 3, 1):
            op = 4 * lax.rem(py + s // 4, 4) + lax.rem(px + s % 4, 4)
            outs[k, s] = pltpu.make_async_remote_copy(
                chunk.at[k, op],
                rows.at[k, p],
                ps_sem.at[k, s],
                pr_sem.at[k, s],
                device_id=(g, op),
                device_id_type=MESH,
            )
            outs[k, s].start()
        rows[k, pl.ds(p, 1)] = chunk[k, pl.ds(p, 1)]

    def along_long(k):
        for s in range(1, 16):
            outs[k, s].wait_recv()
        for grp in range(2):
            turned = rows[k, :, grp].reshape(512, 128).T
            for t in range(4):
                col_c = tlbuf[:, pl.ds(128 * t, 128)]
                col_s = tlbuf[:, pl.ds(512 + 128 * t, 128)]
                both = jnp.dot(turned, jnp.concatenate([col_c, col_s], axis=1), preferred_element_type=F32)
                c = both[:, :128].reshape(8, 2, 8, 128)
                sn = both[:, 128:].reshape(8, 2, 8, 128)
                re = c[:, 0] - sn[:, 1]
                im = c[:, 1] + sn[:, 0]
                rr = frow[k, 0, pl.ds(64 * grp, 64)].reshape(8, 8, 128)
                ri = frow[k, 1, pl.ds(64 * grp, 64)].reshape(8, 8, 128)
                lr = flong[k, 0, :, pl.ds(128 * t, 128)][None]
                li = flong[k, 1, :, pl.ds(128 * t, 128)][None]
                er = rr * lr - ri * li
                ei = rr * li + ri * lr
                out_re = re * er - im * ei
                out_im = re * ei + im * er
                full = jnp.stack([out_re, out_im], axis=1).reshape(2, 2, 2, 16, 128)
                spun = pltpu.roll(full.reshape(128, 128), 64, 1).reshape(2, 2, 2, 16, 128)
                for sign in range(2):
                    at = ((2 * k + grp) * 8 + t) * 2 + sign
                    ff[at] = full[:, sign].reshape(64, 128).astype(jnp.bfloat16)
                    ff[at + 8] = spun[:, sign].reshape(64, 128).astype(jnp.bfloat16)

    def piece(k, lb, gb, high):
        sign = gb >> 2
        grp = (gb & 1) ^ sign
        rot = (lb & 1) if high == 0 else 1 - (lb & 1)
        at = (((2 * k + grp) * 2 + rot) * 4 + (lb >> 1)) * 2 + sign
        return ff[at].astype(F32)

    finals = {}

    def send_pieces(k):
        for s in (8, 9, 7, 6, 10, 11, 5, 4, 12, 13, 3, 2, 14, 15, 1, 0):
            og = 2 * lax.rem(zc + s // 2, 8) + lax.rem(core + s % 2, 2)
            ca = codes[3 * og] >> 2
            cb = codes[3 * og + 1 + k] >> 2
            if k == 0:
                one, two = piece(0, ca >> 3, ca & 7, 0), piece(0, cb >> 3, cb & 7, 1)
            else:
                one, two = piece(1, ca & 7, ca >> 3, 0), piece(1, cb & 7, cb >> 3, 1)
            sb2[k, s] = jnp.where(low, one, two).astype(jnp.bfloat16)
            if s:
                copy = pltpu.make_async_remote_copy(
                    sb2.at[k, s],
                    landing.at[k, g],
                    gs_sem.at[k, s],
                    gr_sem.at[k, s],
                    device_id=(og, p),
                    device_id_type=MESH,
                )
            else:
                copy = pltpu.make_async_copy(sb2.at[k, 0], landing.at[k, g], gs_sem.at[k, 0])
            copy.start()
            finals[k, s] = copy

    for k, n in ((0, 0), (0, 1), (1, 0)):
        hop(k, n)
    tables()
    for k, n in ((0, 2), (0, 3), (1, 1)):
        hop(k, n)
    factors()
    for k, n in ((0, 4), (0, 5), (1, 2), (0, 6), (1, 3), (1, 4)):
        hop(k, n)
    collect(0)
    along_z(0)
    send_lines(0)
    hop(1, 5)
    hop(1, 6)
    collect(1)
    along_z(1)
    send_lines(1)
    loads[5].wait()
    for k in range(2):
        along_long(k)
        send_pieces(k)

    for copy in finals.values():
        copy.wait()
    for copy in outs.values():
        copy.wait_send()
    for copy in hops.values():
        copy.wait_send()
    for copy in swaps.values():
        copy.wait_send()
    kind_copy.wait_send()


def place_kernel(owner_map, landed, order, out, half, f0, d0, k0, sems):
    g = lax.axis_index("grid")
    copies = [pltpu.make_async_copy(landed.at[k], half.at[k], sems.at[k]) for k in range(2)]
    for copy in copies:
        copy.start()
    slot = [jnp.minimum(block_code(owner_map, g, c) & 3, 2) for c in range(3)]
    copies[0].wait()
    f0[...] = half[0].reshape(1024, 128).astype(F32)
    low32 = lax.broadcasted_iota(jnp.int32, (32, 128), 1) < 64
    low8 = low32[:8]
    for q in range(2):
        for z in range(8):
            rows = f0[pl.ds(8 * q + z, 64, stride=16)].astype(jnp.bfloat16)
            buf = z % 2
            d0[buf] = jnp.dot(rows.T, order[...], preferred_element_type=F32)
            for c in range(2):
                even = d0[buf, pl.ds(64 * c, 32, stride=2)]
                odd = d0[buf, pl.ds(64 * c + 1, 32, stride=2)]
                k0[c, q, pl.ds(z, 32, stride=8)] = jnp.where(low32, even, odd)
    copies[1].wait()
    for x2 in range(32):
        ge, ie = (x2, 0) if x2 < 16 else ((0, 1) if x2 == 16 else (32 - x2, 1))
        go, io = (x2, 2) if x2 < 16 else (31 - x2, 3)
        even = half[1, ge, pl.ds(16 * ie, 16)].astype(F32)
        odd = half[1, go, pl.ds(16 * io, 16)].astype(F32)
        for q in range(2):
            e, o = even[8 * q : 8 * q + 8], odd[8 * q : 8 * q + 8]
            first = jnp.where(low8, e, pltpu.roll(o, 64, 1))
            third = jnp.where(low8, pltpu.roll(e, 64, 1), o)
            at = pl.ds(8 * x2, 8)
            cols = pl.ds(128 * x2, 128)
            out[slot[0], q, :, cols] = first + k0[0, q, at]
            out[slot[1], q, :, cols] = k0[1, q, at]
            out[slot[2], q, :, cols] = third


def body(field, levels, coefficients, failed, owner_map, velocity, diffusivity):
    smem = pl.BlockSpec(memory_space=pltpu.SMEM)
    vmem = pl.BlockSpec(memory_space=pltpu.VMEM)
    anyspace = pl.BlockSpec(memory_space=pl.ANY)
    bf = jnp.bfloat16
    dma = pltpu.SemaphoreType.DMA
    landed = pl.pallas_call(
        transform_kernel,
        out_shape=jax.ShapeDtypeStruct((2, 16, 64, 128), bf),
        in_specs=[smem] * 6 + [anyspace] * 5,
        out_specs=anyspace,
        scratch_shapes=[
            pltpu.VMEM((32, 256, 128), bf),
            pltpu.VMEM((256, 256), bf),
            pltpu.VMEM((2, 128, 1024), bf),
            pltpu.VMEM((24, 1, 1024), F32),
            pltpu.VMEM((512, 1024), bf),
            pltpu.VMEM((3, 512, 1024), bf),
            pltpu.VMEM((16, 32, 16, 128), bf),
            pltpu.VMEM((8, 32, 16, 128), bf),
            pltpu.VMEM((2, 16, 128), F32),
            pltpu.VMEM((2, 2, 7, 16, 16, 128), bf),
            pltpu.VMEM((2, 2, 7, 16, 16, 128), bf),
            pltpu.VMEM((2, 512, 128), F32),
            pltpu.VMEM((2, 2, 32, 512), bf),
            pltpu.VMEM((2, 64, 512), bf),
            pltpu.VMEM((2, 16, 2, 32, 128), bf),
            pltpu.VMEM((2, 16, 2, 32, 128), bf),
            pltpu.VMEM((64, 64, 128), bf),
            pltpu.VMEM((2, 16, 64, 128), bf),
            pltpu.VMEM((2, 2, 8, 512), F32),
            pltpu.VMEM((2, 2, 128, 128), F32),
            pltpu.SMEM((48,), jnp.int32),
            dma((6,)), dma((17,)), dma((17,)), dma((2, 2, 7)), dma((2, 2, 7)),
            dma((2, 16)), dma((2, 16)), dma((2, 16)), dma((2, 16)),
        ],
        compiler_params=pltpu.CompilerParams(
            collective_id=0, has_side_effects=True, vmem_limit_bytes=56 * 2**20
        ),
        name="transform",
    )(
        levels, coefficients, failed, owner_map, velocity, diffusivity, field,
        jnp.asarray(mid_table()), jnp.asarray(z_bases()), jnp.asarray(z_masks()), jnp.asarray(long_table()),
    )
    return pl.pallas_call(
        place_kernel,
        out_shape=jax.ShapeDtypeStruct((3, 2, 8, 4096), F32),
        in_specs=[smem, anyspace, vmem],
        out_specs=vmem,
        scratch_shapes=[
            pltpu.VMEM((2, 16, 64, 128), bf),
            pltpu.VMEM((1024, 128), F32),
            pltpu.VMEM((2, 128, 128), F32),
            pltpu.VMEM((2, 2, 256, 128), F32),
            dma((2,)),
        ],
        compiler_params=pltpu.CompilerParams(vmem_limit_bytes=56 * 2**20),
        name="place",
    )(owner_map, landed, jnp.asarray(order_table()))


def solution(mesh):
    placed = (P("grid", "pencil", None, None), P("grid", None), P("grid"), P("grid"), P(), P(), P())
    return jax.shard_map(
        body, mesh=mesh, in_specs=placed, out_specs=P("grid", None, "pencil", None), check_vma=False
    )
```

time: 66.9 us -> 59.4 us (0.89)
  Pallas kernels: 63 us -> 57.9 us
  other arithmetic: 1.3 us -> 0 us
  local copies, waits for them, and re-layouts: 1.04 us -> 0 us
    pallas_call x1, Pallas kernels: 61.1 us -> 54.7 us  [body(): pl.pallas_call(transform_kernel, out_shape=jax.ShapeDtypeStruct((2, 16, 6...]
    pallas_call x1, Pallas kernels: 1.95 us -> 3.2 us  [body(): pl.pallas_call(place_kernel, out_shape=jax.ShapeDtypeStruct((3, 2, 8, 409...]
    unnamed x6 -> x0, local copies, waits for them, and re-layouts: 1.04 us -> none
    select_n x1 -> x0, other arithmetic: 0.67 us -> none  [owner_codes(): key = jnp.where(owner_map >= 0, owner_map // 3 * 3 + kind, -1)]
where the time goes in v3:
time: 59.4 us; the launch traced here: 59.2 us
  Pallas kernels  57.9 us (97%)
  between operations  1.3 us (2%)
    pallas_call x1, Pallas kernels, body(): pl.pallas_call(transform_kernel, out_shape=jax.ShapeDtypeStruct((2, 16, 6...  54.7 us
    pallas_call x1, Pallas kernels, body(): pl.pallas_call(place_kernel, out_shape=jax.ShapeDtypeStruct((3, 2, 8, 409...  3.2 us

profile of v3, /device:TPU:1, one launch (start us, length us, event | category | flops | bytes accessed | tf_op | source)
XLA Modules:
  0.0 59.2 jit_solution(4031023188598510668)
XLA Ops:
  1.3 54.7 %transform.1.landed = bf16[2,16,64,128]{3,2,1,0:T(8,128)(2,1)} custom-call(s32[1,3]{1,0:T(1,128)} %levels.1, s32[1]{0:T(128)S(6)} %copy.13.coefficients, s32[1]{0:T(128)S(6)} %copy.14.failed, s32[64]{0:T(128)} %owner_map.3, f32[3]{0:T(128)} %velocity.1, f32[3]{0:T(128)} %diffusivity.1, bf16[1,32,256,128]{3,2,1,0:T(8,128)(2,1)} %field.1, ...), custom_call_target="tpu_custom_call" | custom-call | tf_op jit(solution)/shard_map/transform/pallas_call | solution.py:468
  56.0 3.2 %place.1 = f32[3,2,8,4096]{3,2,1,0:T(8,128)} custom-call(s32[64]{0:T(128)} %owner_map.3, bf16[2,16,64,128]{3,2,1,0:T(8,128)(2,1)} %transform.1.landed, bf16[64,128]{1,0:T(8,128)(2,1)} %constant.14.clone.order), custom_call_target="tpu_custom_call" | custom-call | tf_op jit(solution)/shard_map/place/pallas_call | solution.py:506

commit v4 on v3

--- a/solution.py
+++ b/solution.py
@@ -106,7 +106,7 @@
     levels, coefficients, failed, owner_map, velocity, diffusivity, field, mid_tab, base_tab, mask_tab, long_tab,
     landing,
     fbuf, tbuf, ebuf, masks, tlbuf, wbuf, v, xr, xk, sb, rz, sf, lhs0, lhs1, chunk, rows, ff, sb2, flong, frow, codes,
-    load_sem, xs_sem, xr_sem, zs_sem, zr_sem, ps_sem, pr_sem, gs_sem, gr_sem,
+    load_sem, xs_sem, xr_sem, zs_sem, zr_sem, ps_sem, pr_sem, gs_sem, gr_sem, row_sem,
 ):
     g = lax.axis_index("grid")
     p = lax.axis_index("pencil")
@@ -125,10 +125,10 @@
         load.start()
 
     barrier = pltpu.get_barrier_semaphore()
-    for s in (8, 9, 6, 7, 10, 11, 4, 5, 12, 13, 2, 3, 14, 15, 1):
+    for s in (2, 14, 1):
         og = 2 * lax.rem(zc + s // 2, 8) + lax.rem(core + s % 2, 2)
         pl.semaphore_signal(barrier, inc=1, device_id=(og, p), device_id_type=MESH)
-    for s in range(1, 16):
+    for s in (4, 8, 12, 1, 2, 3):
         op = 4 * lax.rem(py + s // 4, 4) + lax.rem(px + s % 4, 4)
         pl.semaphore_signal(barrier, inc=1, device_id=(g, op), device_id_type=MESH)
 
@@ -149,14 +149,8 @@
     loads[2].wait()
     lax.fori_loop(8, 16, mid_step, 0)
 
-    def code_step(o, carry):
-        for c in range(3):
-            codes[3 * o + c] = block_code(owner_map, o, c)
-        return carry
-
-    lax.fori_loop(0, 16, code_step, 0)
     xk[0] = jnp.full((16, 128), kind, F32)
-    pl.semaphore_wait(barrier, 30)
+    pl.semaphore_wait(barrier, 9)
 
     mate = (g + 1 - 2 * core, p)
     kind_copy = pltpu.make_async_remote_copy(
@@ -223,6 +217,18 @@
                 device_id_type=MESH,
             )
             hops[k, way, n].start()
+
+    for s in range(1, 4):
+        op = 4 * py + lax.rem(px + s, 4)
+        pl.semaphore_signal(row_sem, inc=1, device_id=(g, op), device_id_type=MESH)
+
+    def find_codes():
+        def code_step(o, carry):
+            for c in range(3):
+                codes[3 * o + c] = block_code(owner_map, o, c)
+            return carry
+
+        lax.fori_loop(0, 16, code_step, 0)
 
     def tables():
         loads[3].wait()
@@ -396,11 +402,15 @@
     tables()
     for k, n in ((0, 2), (0, 3), (1, 1)):
         hop(k, n)
+    find_codes()
+    for k, n in ((0, 4), (0, 5), (1, 2)):
+        hop(k, n)
     factors()
-    for k, n in ((0, 4), (0, 5), (1, 2), (0, 6), (1, 3), (1, 4)):
+    for k, n in ((0, 6), (1, 3), (1, 4)):
         hop(k, n)
     collect(0)
     along_z(0)
+    pl.semaphore_wait(row_sem, 3)
     send_lines(0)
     hop(1, 5)
     hop(1, 6)
@@ -423,12 +433,13 @@
     kind_copy.wait_send()
 
 
-def place_kernel(owner_map, landed, order, out, half, f0, d0, k0, sems):
+def place_kernel(owner_map, landed, order, out, half, f0, d0, k0, staged, sems):
     g = lax.axis_index("grid")
     copies = [pltpu.make_async_copy(landed.at[k], half.at[k], sems.at[k]) for k in range(2)]
     for copy in copies:
         copy.start()
     slot = [jnp.minimum(block_code(owner_map, g, c) & 3, 2) for c in range(3)]
+    puts = [pltpu.make_async_copy(staged.at[c], out.at[slot[c]], sems.at[2 + c]) for c in range(3)]
     copies[0].wait()
     f0[...] = half[0].reshape(1024, 128).astype(F32)
     low32 = lax.broadcasted_iota(jnp.int32, (32, 128), 1) < 64
@@ -436,12 +447,15 @@
     for q in range(2):
         for z in range(8):
             rows = f0[pl.ds(8 * q + z, 64, stride=16)].astype(jnp.bfloat16)
-            buf = z % 2
+            buf = 8 * q + z
             d0[buf] = jnp.dot(rows.T, order[...], preferred_element_type=F32)
             for c in range(2):
                 even = d0[buf, pl.ds(64 * c, 32, stride=2)]
                 odd = d0[buf, pl.ds(64 * c + 1, 32, stride=2)]
                 k0[c, q, pl.ds(z, 32, stride=8)] = jnp.where(low32, even, odd)
+        for x2 in range(32):
+            staged[1, q, :, pl.ds(128 * x2, 128)] = k0[1, q, pl.ds(8 * x2, 8)]
+    puts[1].start()
     copies[1].wait()
     for x2 in range(32):
         ge, ie = (x2, 0) if x2 < 16 else ((0, 1) if x2 == 16 else (32 - x2, 1))
@@ -452,11 +466,13 @@
             e, o = even[8 * q : 8 * q + 8], odd[8 * q : 8 * q + 8]
             first = jnp.where(low8, e, pltpu.roll(o, 64, 1))
             third = jnp.where(low8, pltpu.roll(e, 64, 1), o)
-            at = pl.ds(8 * x2, 8)
             cols = pl.ds(128 * x2, 128)
-            out[slot[0], q, :, cols] = first + k0[0, q, at]
-            out[slot[1], q, :, cols] = k0[1, q, at]
-            out[slot[2], q, :, cols] = third
+            staged[0, q, :, cols] = first + k0[0, q, pl.ds(8 * x2, 8)]
+            staged[2, q, :, cols] = third
+    puts[0].start()
+    puts[2].start()
+    for put in puts:
+        put.wait()
 
 
 def body(field, levels, coefficients, failed, owner_map, velocity, diffusivity):
@@ -494,6 +510,7 @@
             pltpu.SMEM((48,), jnp.int32),
             dma((6,)), dma((17,)), dma((17,)), dma((2, 2, 7)), dma((2, 2, 7)),
             dma((2, 16)), dma((2, 16)), dma((2, 16)), dma((2, 16)),
+            pltpu.SemaphoreType.REGULAR,
         ],
         compiler_params=pltpu.CompilerParams(
             collective_id=0, has_side_effects=True, vmem_limit_bytes=56 * 2**20
@@ -507,13 +524,14 @@
         place_kernel,
         out_shape=jax.ShapeDtypeStruct((3, 2, 8, 4096), F32),
         in_specs=[smem, anyspace, vmem],
-        out_specs=vmem,
+        out_specs=anyspace,
         scratch_shapes=[
             pltpu.VMEM((2, 16, 64, 128), bf),
             pltpu.VMEM((1024, 128), F32),
-            pltpu.VMEM((2, 128, 128), F32),
+            pltpu.VMEM((16, 128, 128), F32),
             pltpu.VMEM((2, 2, 256, 128), F32),
-            dma((2,)),
+            pltpu.VMEM((3, 2, 8, 4096), F32),
+            dma((5,)),
         ],
         compiler_params=pltpu.CompilerParams(vmem_limit_bytes=56 * 2**20),
         name="place",

time: 59.4 us -> 57.6 us (0.970)
  Pallas kernels: 57.9 us -> 56.1 us
    pallas_call x1, Pallas kernels: 54.7 us -> 53 us  [body(): pl.pallas_call(transform_kernel, out_shape=jax.ShapeDtypeStruct((2, 16, 6...]
where the time goes in v4:
time: 57.6 us; the launch traced here: 57.4 us
  Pallas kernels  56.1 us (97%)
  between operations  1.3 us (2%)
    pallas_call x1, Pallas kernels, body(): pl.pallas_call(transform_kernel, out_shape=jax.ShapeDtypeStruct((2, 16, 6...  53 us
    pallas_call x1, Pallas kernels, body(): pl.pallas_call(place_kernel, out_shape=jax.ShapeDtypeStruct((3, 2, 8, 409...  3.13 us

profile of v4, /device:TPU:1, one launch (start us, length us, event | category | flops | bytes accessed | tf_op | source)
XLA Modules:
  0.0 57.4 jit_solution(17044433360958215725)
XLA Ops:
  1.3 53.0 %transform.1.landed = bf16[2,16,64,128]{3,2,1,0:T(8,128)(2,1)} custom-call(s32[1,3]{1,0:T(1,128)} %levels.1, s32[1]{0:T(128)S(6)} %copy.13.coefficients, s32[1]{0:T(128)S(6)} %copy.14.failed, s32[64]{0:T(128)} %owner_map.3, f32[3]{0:T(128)} %velocity.1, f32[3]{0:T(128)} %diffusivity.1, bf16[1,32,256,128]{3,2,1,0:T(8,128)(2,1)} %field.1, ...), custom_call_target="tpu_custom_call" | custom-call | tf_op jit(solution)/shard_map/transform/pallas_call | solution.py:484
  54.3 3.1 %place.1 = f32[3,2,8,4096]{3,2,1,0:T(8,128)} custom-call(s32[64]{0:T(128)} %owner_map.3, bf16[2,16,64,128]{3,2,1,0:T(8,128)(2,1)} %transform.1.landed, bf16[64,128]{1,0:T(8,128)(2,1)} %constant.14.clone.order), custom_call_target="tpu_custom_call" | custom-call | tf_op jit(solution)/shard_map/place/pallas_call | solution.py:523

commit v5 on v4

--- a/solution.py
+++ b/solution.py
@@ -145,9 +145,9 @@
         return carry
 
     loads[1].wait()
-    lax.fori_loop(0, 8, mid_step, 0)
+    lax.fori_loop(0, 8, mid_step, 0, unroll=4)
     loads[2].wait()
-    lax.fori_loop(8, 16, mid_step, 0)
+    lax.fori_loop(8, 16, mid_step, 0, unroll=4)
 
     xk[0] = jnp.full((16, 128), kind, F32)
     pl.semaphore_wait(barrier, 9)

time: 57.6 us -> 55.8 us (0.969)
  Pallas kernels: 56.1 us -> 54.3 us
    pallas_call x1, Pallas kernels: 53 us -> 51.2 us  [body(): pl.pallas_call(transform_kernel, out_shape=jax.ShapeDtypeStruct((2, 16, 6...]
where the time goes in v5:
time: 55.8 us; the launch traced here: 55.6 us
  Pallas kernels  54.3 us (97%)
  between operations  1.3 us (2%)
    pallas_call x1, Pallas kernels, body(): pl.pallas_call(transform_kernel, out_shape=jax.ShapeDtypeStruct((2, 16, 6...  51.2 us
    pallas_call x1, Pallas kernels, body(): pl.pallas_call(place_kernel, out_shape=jax.ShapeDtypeStruct((3, 2, 8, 409...  3.13 us

profile of v5, /device:TPU:1, one launch (start us, length us, event | category | flops | bytes accessed | tf_op | source)
XLA Modules:
  0.0 55.6 jit_solution(2301678119391168389)
XLA Ops:
  1.3 51.2 %transform.1.landed = bf16[2,16,64,128]{3,2,1,0:T(8,128)(2,1)} custom-call(s32[1,3]{1,0:T(1,128)} %levels.1, s32[1]{0:T(128)S(6)} %copy.13.coefficients, s32[1]{0:T(128)S(6)} %copy.14.failed, s32[64]{0:T(128)} %owner_map.3, f32[3]{0:T(128)} %velocity.1, f32[3]{0:T(128)} %diffusivity.1, bf16[1,32,256,128]{3,2,1,0:T(8,128)(2,1)} %field.1, ...), custom_call_target="tpu_custom_call" | custom-call | tf_op jit(solution)/shard_map/transform/pallas_call | solution.py:484
  52.5 3.1 %place.1 = f32[3,2,8,4096]{3,2,1,0:T(8,128)} custom-call(s32[64]{0:T(128)} %owner_map.3, bf16[2,16,64,128]{3,2,1,0:T(8,128)(2,1)} %transform.1.landed, bf16[64,128]{1,0:T(8,128)(2,1)} %constant.14.clone.order), custom_call_target="tpu_custom_call" | custom-call | tf_op jit(solution)/shard_map/place/pallas_call | solution.py:523

commit v6 on v5

--- a/solution.py
+++ b/solution.py
@@ -170,7 +170,8 @@
             device_id=mate,
             device_id_type=MESH,
         )
-        swaps[d, h].start()
+        if len(swaps) <= 4:
+            swaps[d, h].start()
     kind_copy.wait_recv()
     other = xk[1][None]
     mine = kind
@@ -397,7 +398,10 @@
             copy.start()
             finals[k, s] = copy
 
-    for k, n in ((0, 0), (0, 1), (1, 0)):
+    hop(0, 0)
+    for d, h in order[4:]:
+        swaps[d, h].start()
+    for k, n in ((0, 1), (1, 0)):
         hop(k, n)
     tables()
     for k, n in ((0, 2), (0, 3), (1, 1)):

time: 55.8 us -> 55.8 us (level)
  no operation moved by 1% of the time
where the time goes in v6:
time: 55.8 us; the launch traced here: 55.6 us
  Pallas kernels  54.3 us (97%)
  between operations  1.3 us (2%)
    pallas_call x1, Pallas kernels, body(): pl.pallas_call(transform_kernel, out_shape=jax.ShapeDtypeStruct((2, 16, 6...  51.2 us
    pallas_call x1, Pallas kernels, body(): pl.pallas_call(place_kernel, out_shape=jax.ShapeDtypeStruct((3, 2, 8, 409...  3.13 us

profile of v6, /device:TPU:1, one launch (start us, length us, event | category | flops | bytes accessed | tf_op | source)
XLA Modules:
  0.0 55.6 jit_solution(17617240850068338266)
XLA Ops:
  1.3 51.2 %transform.1.landed = bf16[2,16,64,128]{3,2,1,0:T(8,128)(2,1)} custom-call(s32[1,3]{1,0:T(1,128)} %levels.1, s32[1]{0:T(128)S(6)} %copy.13.coefficients, s32[1]{0:T(128)S(6)} %copy.14.failed, s32[64]{0:T(128)} %owner_map.3, f32[3]{0:T(128)} %velocity.1, f32[3]{0:T(128)} %diffusivity.1, bf16[1,32,256,128]{3,2,1,0:T(8,128)(2,1)} %field.1, ...), custom_call_target="tpu_custom_call" | custom-call | tf_op jit(solution)/shard_map/transform/pallas_call | solution.py:488
  52.5 3.1 %place.1 = f32[3,2,8,4096]{3,2,1,0:T(8,128)} custom-call(s32[64]{0:T(128)} %owner_map.3, bf16[2,16,64,128]{3,2,1,0:T(8,128)(2,1)} %transform.1.landed, bf16[64,128]{1,0:T(8,128)(2,1)} %constant.14.clone.order), custom_call_target="tpu_custom_call" | custom-call | tf_op jit(solution)/shard_map/place/pallas_call | solution.py:527
